TPU v7x, 128 devices: a whole 4x4x4 slice. The times are simulated.
128 devices in a mesh: ctx: 8 (over y, z_hi), head: 4 (over z_lo, core), dp: 4 (over x).
Axes of the slice: x: 4, y: 4, z: 4 (z_hi: 2, z_lo: 2; z = z_hi * 2 + z_lo), core: 2. Of those that a mesh axis runs over, the one named last changes fastest.
Arguments:
- long_query: bfloat16 [24576, 8192], P(('dp', 'ctx', 'head')), parts along dimension 0, may hold values from -250 to 250
- long_kv: bfloat16 [2, 24576, 1024], P(None, ('dp', 'ctx', 'head')), parts along dimension 1, may hold values from -250 to 250
- short_query: bfloat16 [32768, 8192], P(('dp', 'ctx', 'head')), parts along dimension 0, may hold values from -250 to 250
- short_key_value: bfloat16 [2, 32768, 1024], P(None, ('dp', 'ctx', 'head')), parts along dimension 1, may hold values from -250 to 250
- short_seg: int32 [128, 256], P(('dp', 'ctx', 'head')), parts along dimension 0, may hold values from 0 to 7, never falling along the last dimension, each value on 1 to 128 neighbouring positions
Outputs:
- long_out: bfloat16 [24576, 8192], P(('dp', 'ctx', 'head')), parts along dimension 0
- short_out: bfloat16 [32768, 8192], P(('dp', 'ctx', 'head')), parts along dimension 0
There are 4 independent parts, one for each index of `dp`. A program takes and returns all parts, laid end to end along the dimension named above; each array names one. Nothing has to cross between parts.
All inputs are finite; a program needn't handle non-finite values.
Results may differ from a plain program's by a relative error of at most 0.0035.
Values may be sent and summed in bfloat16 or wider, within the bound.
A program may use at most 256 MiB of HBM per device.

v0:
```python
import math

import jax
import jax.numpy as jnp
from jax import lax
from jax.sharding import PartitionSpec as P

QUERY_HEAD_COUNT = 64
KEY_VALUE_HEADS = 8
HEAD_SIZE = 128


NEG_LARGE = -1e30


def blank_state(count_of_rows, kv_heads, head_groups):
    highest = jnp.full((kv_heads, head_groups, count_of_rows), NEG_LARGE, jnp.float32)
    totals = jnp.zeros((kv_heads, head_groups, count_of_rows), jnp.float32)
    accum = jnp.zeros((kv_heads, head_groups, count_of_rows, HEAD_SIZE), jnp.float32)
    return (highest, totals, accum)


def update_state(softmax_state, query_rows, stacked_rows, allowed):
    running_max, totals, accum = softmax_state
    kv_heads = query_rows.shape[1]
    head_dim = query_rows.shape[3]
    key_part = stacked_rows[0].reshape(stacked_rows.shape[1], kv_heads, head_dim)
    value_part = stacked_rows[1].reshape(stacked_rows.shape[1], kv_heads, head_dim)
    scores = jnp.einsum(
        "tkgd,skd->kgts", query_rows, key_part, preferred_element_type=jnp.float32
    ) * (1.0 / math.sqrt(head_dim))
    masked = jnp.where(allowed, scores, NEG_LARGE)
    new_max = jnp.maximum(running_max, jnp.max(masked, axis=-1))
    factor = jnp.exp(running_max - new_max)
    weights = jnp.where(allowed, jnp.exp(scores - new_max[..., None]), 0.0)
    totals = totals * factor + jnp.sum(weights, axis=-1)
    accum = accum * factor[..., None] + jnp.einsum(
        "kgts,skd->kgtd",
        weights.astype(jnp.bfloat16),
        value_part,
        preferred_element_type=jnp.float32,
    )
    return (new_max, totals, accum)


def finish_state(softmax_state):
    running_max, totals, accum = softmax_state
    mixed = (accum / totals[..., None]).astype(jnp.bfloat16)
    return mixed.transpose(2, 0, 1, 3).reshape(mixed.shape[2], -1)


def fold_long(query_rows, query_pos, block_length):

    def fold_step(running, shard_piece, begin_at):
        turns = shard_piece.shape[1] // block_length

        def one_turn(turn_index, inner_state):
            offset = begin_at + turn_index * block_length
            part_kv = lax.dynamic_slice_in_dim(
                shard_piece, turn_index * block_length, block_length, 1
            )
            key_pos = offset + jnp.arange(block_length, dtype=jnp.int32)
            allowed = key_pos[None, :] <= query_pos[:, None]
            return lax.cond(
                offset <= query_pos[-1],
                lambda held_state: update_state(held_state, query_rows, part_kv, allowed),
                lambda held_state: held_state,
                inner_state,
            )

        return lax.fori_loop(0, turns, one_turn, running)

    return fold_step


def attend_short(short_query, short_key_value, short_seg):
    sequence_length = short_query.shape[0]
    head_groups = QUERY_HEAD_COUNT // KEY_VALUE_HEADS
    query_rows = short_query.reshape(sequence_length, KEY_VALUE_HEADS, head_groups, HEAD_SIZE)
    labels = short_seg[0]
    positions = jnp.arange(sequence_length, dtype=jnp.int32)
    block_length = sequence_length // 4
    pieces_out = []
    for query_block in range(4):
        query_low = query_block * block_length
        query_high = query_low + block_length
        softmax_state = blank_state(block_length, KEY_VALUE_HEADS, head_groups)
        for key_block in range(query_block + 1):
            key_low = key_block * block_length
            key_high = key_low + block_length
            allowed = (
                positions[key_low:key_high][None, :] <= positions[query_low:query_high][:, None]
            ) & (labels[key_low:key_high][None, :] == labels[query_low:query_high][:, None])
            softmax_state = update_state(
                softmax_state,
                query_rows[query_low:query_high],
                short_key_value[:, key_low:key_high],
                allowed,
            )
        pieces_out.append(finish_state(softmax_state))
    return jnp.concatenate(pieces_out, axis=0)


def on_device(long_query, long_kv, short_query, short_key_value, short_seg):
    token_rows = long_query.shape[0]
    head_groups = QUERY_HEAD_COUNT // KEY_VALUE_HEADS
    window_count = lax.axis_size("ctx") * lax.axis_size("head")
    flat_rank = lax.axis_index("ctx") * lax.axis_size("head") + lax.axis_index("head")
    query_rows = long_query.reshape(token_rows, KEY_VALUE_HEADS, head_groups, HEAD_SIZE)
    query_pos = flat_rank * token_rows + jnp.arange(token_rows, dtype=jnp.int32)
    shards_per_block = 1
    while shards_per_block * token_rows < 512 and shards_per_block < window_count:
        shards_per_block = shards_per_block * 2
    gathered = lax.all_gather(long_kv, ("ctx", "head"), axis=1, tiled=True)
    fold_step = fold_long(query_rows, query_pos, shards_per_block * token_rows)
    softmax_state = fold_step(blank_state(token_rows, KEY_VALUE_HEADS, head_groups), gathered, 0)
    long_out = finish_state(softmax_state)
    short_out = attend_short(short_query, short_key_value, short_seg)
    return (long_out, short_out)


def solution(mesh):
    return jax.shard_map(
        on_device,
        mesh=mesh,
        in_specs=(
            P(("dp", "ctx", "head"), None),
            P(None, ("dp", "ctx", "head"), None),
            P(("dp", "ctx", "head"), None),
            P(None, ("dp", "ctx", "head"), None),
            P(("dp", "ctx", "head"), None),
        ),
        out_specs=(P(("dp", "ctx", "head"), None), P(("dp", "ctx", "head"), None)),
        check_vma=False,
    )
```

profile of v0, /device:TPU:89, one launch (start us, length us, event | category | flops | bytes accessed | tf_op | source)
XLA Modules:
  0.0 643.4 jit_solution(1320893152180307649)
XLA Ops:
  7.2 2.8 copy.69
  10.1 2.8 copy.193
  12.9 3.7 copy.71
  30.8 3.9 fusion.14
  48.9 3.0 fusion.31
  57.3 2.4 fusion.44
  61.1 1.9 fusion.53
  63.7 1.8 copy.320
  65.5 3.2 pad_maximum_fusion
  68.7 33.4 %all-gather.2.cloned.1.call-done = bf16[2,6144,1024]{2,0,1:T(2,128)(2,1)} async-done(((bf16[2,192,1024]{2,0,1:T(2,128)(2,1)}), bf16[2,6144,1024]{2,0,1:T(2,128)(2,1)}) %all-gather.2.cloned.1.call-update) | async-done | bytes 25165840 | tf_op jit(solution)/shard_map/all_gather | solution.py:114
  102.1 60.8 %copy.70 = bf16[2,6144,1024]{1,2,0:T(8,128)(2,1)} copy(bf16[2,6144,1024]{2,0,1:T(2,128)(2,1)} %all-gather.2.cloned.1.call-done) | data formatting | bytes 50331648 | tf_op jit(solution)/shard_map/while | solution.py:71
  162.9 3.4 broadcast_in_dim.168
  166.3 458.5 %while.17 = (s32[]{:T(128)}, f32[8,8,192]{2,1,0:T(8,128)S(1)}, f32[8,8,192]{2,1,0:T(8,128)S(1)}, f32[8,8,192,128]{3,2,1,0:T(8,128)}, s32[192]{0:T(256)S(1)}, /*i...) while((s32[]{:T(128)}, f32[8,8,192]{2,1,0:T(8,128)S(1)}, ...), condition=%wide.region_5.6_spmd, body=%wide.region_0.5_spmd.sunk | while | flops 4938966016 | bytes 190133392 | solution.py:71
  167.9 55.9 %conditional.2 = ((f32[8,8,192]{2,1,0:T(8,128)S(1)}, f32[8,8,192]{2,1,0:T(8,128)S(1)}, f32[8,8,192,128]{3,2,1,0:T(8,128)})) conditional(s32[]{:T(128)} %convert_element_type.108, (f32[8,8,192]{2,1,0:T(8,128)S(1)}, f32[8,8,192]{2,1,0:T(8,128)S(1)}, f32[8,8,192,128]{3,2,1,0:T(8,128)}) %tuple.107, (s32[]{:T(128)}, s32[1,768]{1,0:T(1,128)S(1)}, ...), branch_computations={%region_1.0_spmd, %region_2.4_spmd} | conditional | flops 4938966016 | bytes 190130080 | solution.py:64
  168.1 2.1 constant_dynamic-slice_fusion.1
  170.2 17.2 %fusion = (f32[8,8,192]{2,1,0:T(8,128)S(1)}, f32[8,768,192,8]{1,2,3,0:T(8,128)}) fusion(pred[192,768]{1,0:T(8,128)(4,1)S(1)} %broadcast_compare_fusion, bf16[768,8,128,1]{0,2,3,1:T(8,128)(2,1)S(1)} %bitcast.483, bf16[192,8,8,128]{3,0,2,1:T(8,128)(2,1)} %get-tuple-element.211), kind=kOutput, calls=%fused_computation.2 | convolution fusion | flops 2444218368 | bytes 42663936 | tf_op jit(solution)/shard_map/while/body/eval_jaxpr/cond/branch_1_fun/tkgd,skd->kgts/dot_general | solution.py:29
  187.4 17.0 %fusion.4 = f32[8,8,192]{2,1,0:T(8,128)S(1)} fusion(f32[8,768,192,8]{1,2,3,0:T(8,128)} %get-tuple-element.276, f32[8,8,192]{2,1,0:T(8,128)S(1)} %max.122, pred[192,768]{1,0:T(8,128)(4,1)S(1)} %broadcast_compare_fusion), kind=kLoop, calls=%fused_computation.6 | loop fusion | flops 37736448 | bytes 37994496 | tf_op jit(solution)/shard_map/while/body/eval_jaxpr/cond/branch_1_fun/reduce_sum | solution.py:36
  204.4 16.7 %multiply_add_fusion = f32[8,8,192,128]{3,2,1,0:T(8,128)S(1)} fusion(f32[8,8,192,128]{3,2,1,0:T(8,128)S(1)} %copy-done, f32[8,8,192]{2,1,0:T(8,128)S(1)} %get-tuple-element.260, bf16[768,8,128,1]{0,2,3,1:T(8,128)(2,1)S(1)} %bitcast.484, f32[8,768,192,8]{1,2,3,0:T(8,128)} %get-tuple-element.276, f32[8,8,192]{2,1,0:T(8,128)S(1)} %max.122, ...), kind=kOutput, calls=%fused_computation.9 | convolution fusion | flops 2456813568 | bytes 52150272 | tf_op jit(solution)/shard_map/while/body/eval_jaxpr/cond/branch_1_fun/kgts,skd->kgtd/dot_general | solution.py:37
  221.2 2.6 copy-done.1
  225.1 55.9 %conditional.2 = ((f32[8,8,192]{2,1,0:T(8,128)S(1)}, f32[8,8,192]{2,1,0:T(8,128)S(1)}, f32[8,8,192,128]{3,2,1,0:T(8,128)})) conditional(s32[]{:T(128)} %convert_element_type.108, (f32[8,8,192]{2,1,0:T(8,128)S(1)}, f32[8,8,192]{2,1,0:T(8,128)S(1)}, f32[8,8,192,128]{3,2,1,0:T(8,128)}) %tuple.107, (s32[]{:T(128)}, s32[1,768]{1,0:T(1,128)S(1)}, ...), branch_computations={%region_1.0_spmd, %region_2.4_spmd} | conditional | flops 4938966016 | bytes 190130080 | solution.py:64
  225.4 2.1 constant_dynamic-slice_fusion.1
  227.5 17.2 %fusion = (f32[8,8,192]{2,1,0:T(8,128)S(1)}, f32[8,768,192,8]{1,2,3,0:T(8,128)}) fusion(pred[192,768]{1,0:T(8,128)(4,1)S(1)} %broadcast_compare_fusion, bf16[768,8,128,1]{0,2,3,1:T(8,128)(2,1)S(1)} %bitcast.483, bf16[192,8,8,128]{3,0,2,1:T(8,128)(2,1)} %get-tuple-element.211), kind=kOutput, calls=%fused_computation.2 | convolution fusion | flops 2444218368 | bytes 42663936 | tf_op jit(solution)/shard_map/while/body/eval_jaxpr/cond/branch_1_fun/tkgd,skd->kgts/dot_general | solution.py:29
  244.6 17.0 %fusion.4 = f32[8,8,192]{2,1,0:T(8,128)S(1)} fusion(f32[8,768,192,8]{1,2,3,0:T(8,128)} %get-tuple-element.276, f32[8,8,192]{2,1,0:T(8,128)S(1)} %max.122, pred[192,768]{1,0:T(8,128)(4,1)S(1)} %broadcast_compare_fusion), kind=kLoop, calls=%fused_computation.6 | loop fusion | flops 37736448 | bytes 37994496 | tf_op jit(solution)/shard_map/while/body/eval_jaxpr/cond/branch_1_fun/reduce_sum | solution.py:36
  261.7 16.7 %multiply_add_fusion = f32[8,8,192,128]{3,2,1,0:T(8,128)S(1)} fusion(f32[8,8,192,128]{3,2,1,0:T(8,128)S(1)} %copy-done, f32[8,8,192]{2,1,0:T(8,128)S(1)} %get-tuple-element.260, bf16[768,8,128,1]{0,2,3,1:T(8,128)(2,1)S(1)} %bitcast.484, f32[8,768,192,8]{1,2,3,0:T(8,128)} %get-tuple-element.276, f32[8,8,192]{2,1,0:T(8,128)S(1)} %max.122, ...), kind=kOutput, calls=%fused_computation.9 | convolution fusion | flops 2456813568 | bytes 52150272 | tf_op jit(solution)/shard_map/while/body/eval_jaxpr/cond/branch_1_fun/kgts,skd->kgtd/dot_general | solution.py:37
  278.5 2.6 copy-done.1
  282.4 55.9 %conditional.2 = ((f32[8,8,192]{2,1,0:T(8,128)S(1)}, f32[8,8,192]{2,1,0:T(8,128)S(1)}, f32[8,8,192,128]{3,2,1,0:T(8,128)})) conditional(s32[]{:T(128)} %convert_element_type.108, (f32[8,8,192]{2,1,0:T(8,128)S(1)}, f32[8,8,192]{2,1,0:T(8,128)S(1)}, f32[8,8,192,128]{3,2,1,0:T(8,128)}) %tuple.107, (s32[]{:T(128)}, s32[1,768]{1,0:T(1,128)S(1)}, ...), branch_computations={%region_1.0_spmd, %region_2.4_spmd} | conditional | flops 4938966016 | bytes 190130080 | solution.py:64
  282.6 2.1 constant_dynamic-slice_fusion.1
  284.7 17.2 %fusion = (f32[8,8,192]{2,1,0:T(8,128)S(1)}, f32[8,768,192,8]{1,2,3,0:T(8,128)}) fusion(pred[192,768]{1,0:T(8,128)(4,1)S(1)} %broadcast_compare_fusion, bf16[768,8,128,1]{0,2,3,1:T(8,128)(2,1)S(1)} %bitcast.483, bf16[192,8,8,128]{3,0,2,1:T(8,128)(2,1)} %get-tuple-element.211), kind=kOutput, calls=%fused_computation.2 | convolution fusion | flops 2444218368 | bytes 42663936 | tf_op jit(solution)/shard_map/while/body/eval_jaxpr/cond/branch_1_fun/tkgd,skd->kgts/dot_general | solution.py:29
  301.9 17.0 %fusion.4 = f32[8,8,192]{2,1,0:T(8,128)S(1)} fusion(f32[8,768,192,8]{1,2,3,0:T(8,128)} %get-tuple-element.276, f32[8,8,192]{2,1,0:T(8,128)S(1)} %max.122, pred[192,768]{1,0:T(8,128)(4,1)S(1)} %broadcast_compare_fusion), kind=kLoop, calls=%fused_computation.6 | loop fusion | flops 37736448 | bytes 37994496 | tf_op jit(solution)/shard_map/while/body/eval_jaxpr/cond/branch_1_fun/reduce_sum | solution.py:36
  319.0 16.7 %multiply_add_fusion = f32[8,8,192,128]{3,2,1,0:T(8,128)S(1)} fusion(f32[8,8,192,128]{3,2,1,0:T(8,128)S(1)} %copy-done, f32[8,8,192]{2,1,0:T(8,128)S(1)} %get-tuple-element.260, bf16[768,8,128,1]{0,2,3,1:T(8,128)(2,1)S(1)} %bitcast.484, f32[8,768,192,8]{1,2,3,0:T(8,128)} %get-tuple-element.276, f32[8,8,192]{2,1,0:T(8,128)S(1)} %max.122, ...), kind=kOutput, calls=%fused_computation.9 | convolution fusion | flops 2456813568 | bytes 52150272 | tf_op jit(solution)/shard_map/while/body/eval_jaxpr/cond/branch_1_fun/kgts,skd->kgtd/dot_general | solution.py:37
  335.7 2.6 copy-done.1
  339.7 55.9 %conditional.2 = ((f32[8,8,192]{2,1,0:T(8,128)S(1)}, f32[8,8,192]{2,1,0:T(8,128)S(1)}, f32[8,8,192,128]{3,2,1,0:T(8,128)})) conditional(s32[]{:T(128)} %convert_element_type.108, (f32[8,8,192]{2,1,0:T(8,128)S(1)}, f32[8,8,192]{2,1,0:T(8,128)S(1)}, f32[8,8,192,128]{3,2,1,0:T(8,128)}) %tuple.107, (s32[]{:T(128)}, s32[1,768]{1,0:T(1,128)S(1)}, ...), branch_computations={%region_1.0_spmd, %region_2.4_spmd} | conditional | flops 4938966016 | bytes 190130080 | solution.py:64
  339.9 2.1 constant_dynamic-slice_fusion.1
  342.0 17.2 %fusion = (f32[8,8,192]{2,1,0:T(8,128)S(1)}, f32[8,768,192,8]{1,2,3,0:T(8,128)}) fusion(pred[192,768]{1,0:T(8,128)(4,1)S(1)} %broadcast_compare_fusion, bf16[768,8,128,1]{0,2,3,1:T(8,128)(2,1)S(1)} %bitcast.483, bf16[192,8,8,128]{3,0,2,1:T(8,128)(2,1)} %get-tuple-element.211), kind=kOutput, calls=%fused_computation.2 | convolution fusion | flops 2444218368 | bytes 42663936 | tf_op jit(solution)/shard_map/while/body/eval_jaxpr/cond/branch_1_fun/tkgd,skd->kgts/dot_general | solution.py:29
  359.2 17.0 %fusion.4 = f32[8,8,192]{2,1,0:T(8,128)S(1)} fusion(f32[8,768,192,8]{1,2,3,0:T(8,128)} %get-tuple-element.276, f32[8,8,192]{2,1,0:T(8,128)S(1)} %max.122, pred[192,768]{1,0:T(8,128)(4,1)S(1)} %broadcast_compare_fusion), kind=kLoop, calls=%fused_computation.6 | loop fusion | flops 37736448 | bytes 37994496 | tf_op jit(solution)/shard_map/while/body/eval_jaxpr/cond/branch_1_fun/reduce_sum | solution.py:36
  376.3 16.7 %multiply_add_fusion = f32[8,8,192,128]{3,2,1,0:T(8,128)S(1)} fusion(f32[8,8,192,128]{3,2,1,0:T(8,128)S(1)} %copy-done, f32[8,8,192]{2,1,0:T(8,128)S(1)} %get-tuple-element.260, bf16[768,8,128,1]{0,2,3,1:T(8,128)(2,1)S(1)} %bitcast.484, f32[8,768,192,8]{1,2,3,0:T(8,128)} %get-tuple-element.276, f32[8,8,192]{2,1,0:T(8,128)S(1)} %max.122, ...), kind=kOutput, calls=%fused_computation.9 | convolution fusion | flops 2456813568 | bytes 52150272 | tf_op jit(solution)/shard_map/while/body/eval_jaxpr/cond/branch_1_fun/kgts,skd->kgtd/dot_general | solution.py:37
  393.0 2.6 copy-done.1
  397.0 55.9 %conditional.2 = ((f32[8,8,192]{2,1,0:T(8,128)S(1)}, f32[8,8,192]{2,1,0:T(8,128)S(1)}, f32[8,8,192,128]{3,2,1,0:T(8,128)})) conditional(s32[]{:T(128)} %convert_element_type.108, (f32[8,8,192]{2,1,0:T(8,128)S(1)}, f32[8,8,192]{2,1,0:T(8,128)S(1)}, f32[8,8,192,128]{3,2,1,0:T(8,128)}) %tuple.107, (s32[]{:T(128)}, s32[1,768]{1,0:T(1,128)S(1)}, ...), branch_computations={%region_1.0_spmd, %region_2.4_spmd} | conditional | flops 4938966016 | bytes 190130080 | solution.py:64
  397.2 2.1 constant_dynamic-slice_fusion.1
  399.3 17.2 %fusion = (f32[8,8,192]{2,1,0:T(8,128)S(1)}, f32[8,768,192,8]{1,2,3,0:T(8,128)}) fusion(pred[192,768]{1,0:T(8,128)(4,1)S(1)} %broadcast_compare_fusion, bf16[768,8,128,1]{0,2,3,1:T(8,128)(2,1)S(1)} %bitcast.483, bf16[192,8,8,128]{3,0,2,1:T(8,128)(2,1)} %get-tuple-element.211), kind=kOutput, calls=%fused_computation.2 | convolution fusion | flops 2444218368 | bytes 42663936 | tf_op jit(solution)/shard_map/while/body/eval_jaxpr/cond/branch_1_fun/tkgd,skd->kgts/dot_general | solution.py:29
  416.5 17.0 %fusion.4 = f32[8,8,192]{2,1,0:T(8,128)S(1)} fusion(f32[8,768,192,8]{1,2,3,0:T(8,128)} %get-tuple-element.276, f32[8,8,192]{2,1,0:T(8,128)S(1)} %max.122, pred[192,768]{1,0:T(8,128)(4,1)S(1)} %broadcast_compare_fusion), kind=kLoop, calls=%fused_computation.6 | loop fusion | flops 37736448 | bytes 37994496 | tf_op jit(solution)/shard_map/while/body/eval_jaxpr/cond/branch_1_fun/reduce_sum | solution.py:36
  433.6 16.7 %multiply_add_fusion = f32[8,8,192,128]{3,2,1,0:T(8,128)S(1)} fusion(f32[8,8,192,128]{3,2,1,0:T(8,128)S(1)} %copy-done, f32[8,8,192]{2,1,0:T(8,128)S(1)} %get-tuple-element.260, bf16[768,8,128,1]{0,2,3,1:T(8,128)(2,1)S(1)} %bitcast.484, f32[8,768,192,8]{1,2,3,0:T(8,128)} %get-tuple-element.276, f32[8,8,192]{2,1,0:T(8,128)S(1)} %max.122, ...), kind=kOutput, calls=%fused_computation.9 | convolution fusion | flops 2456813568 | bytes 52150272 | tf_op jit(solution)/shard_map/while/body/eval_jaxpr/cond/branch_1_fun/kgts,skd->kgtd/dot_general | solution.py:37
  450.3 2.6 copy-done.1
  454.3 55.9 %conditional.2 = ((f32[8,8,192]{2,1,0:T(8,128)S(1)}, f32[8,8,192]{2,1,0:T(8,128)S(1)}, f32[8,8,192,128]{3,2,1,0:T(8,128)})) conditional(s32[]{:T(128)} %convert_element_type.108, (f32[8,8,192]{2,1,0:T(8,128)S(1)}, f32[8,8,192]{2,1,0:T(8,128)S(1)}, f32[8,8,192,128]{3,2,1,0:T(8,128)}) %tuple.107, (s32[]{:T(128)}, s32[1,768]{1,0:T(1,128)S(1)}, ...), branch_computations={%region_1.0_spmd, %region_2.4_spmd} | conditional | flops 4938966016 | bytes 190130080 | solution.py:64
  454.5 2.1 constant_dynamic-slice_fusion.1
  456.6 17.2 %fusion = (f32[8,8,192]{2,1,0:T(8,128)S(1)}, f32[8,768,192,8]{1,2,3,0:T(8,128)}) fusion(pred[192,768]{1,0:T(8,128)(4,1)S(1)} %broadcast_compare_fusion, bf16[768,8,128,1]{0,2,3,1:T(8,128)(2,1)S(1)} %bitcast.483, bf16[192,8,8,128]{3,0,2,1:T(8,128)(2,1)} %get-tuple-element.211), kind=kOutput, calls=%fused_computation.2 | convolution fusion | flops 2444218368 | bytes 42663936 | tf_op jit(solution)/shard_map/while/body/eval_jaxpr/cond/branch_1_fun/tkgd,skd->kgts/dot_general | solution.py:29
  473.8 17.0 %fusion.4 = f32[8,8,192]{2,1,0:T(8,128)S(1)} fusion(f32[8,768,192,8]{1,2,3,0:T(8,128)} %get-tuple-element.276, f32[8,8,192]{2,1,0:T(8,128)S(1)} %max.122, pred[192,768]{1,0:T(8,128)(4,1)S(1)} %broadcast_compare_fusion), kind=kLoop, calls=%fused_computation.6 | loop fusion | flops 37736448 | bytes 37994496 | tf_op jit(solution)/shard_map/while/body/eval_jaxpr/cond/branch_1_fun/reduce_sum | solution.py:36
  490.8 16.7 %multiply_add_fusion = f32[8,8,192,128]{3,2,1,0:T(8,128)S(1)} fusion(f32[8,8,192,128]{3,2,1,0:T(8,128)S(1)} %copy-done, f32[8,8,192]{2,1,0:T(8,128)S(1)} %get-tuple-element.260, bf16[768,8,128,1]{0,2,3,1:T(8,128)(2,1)S(1)} %bitcast.484, f32[8,768,192,8]{1,2,3,0:T(8,128)} %get-tuple-element.276, f32[8,8,192]{2,1,0:T(8,128)S(1)} %max.122, ...), kind=kOutput, calls=%fused_computation.9 | convolution fusion | flops 2456813568 | bytes 52150272 | tf_op jit(solution)/shard_map/while/body/eval_jaxpr/cond/branch_1_fun/kgts,skd->kgtd/dot_general | solution.py:37
  507.6 2.6 copy-done.1
  511.6 55.9 %conditional.2 = ((f32[8,8,192]{2,1,0:T(8,128)S(1)}, f32[8,8,192]{2,1,0:T(8,128)S(1)}, f32[8,8,192,128]{3,2,1,0:T(8,128)})) conditional(s32[]{:T(128)} %convert_element_type.108, (f32[8,8,192]{2,1,0:T(8,128)S(1)}, f32[8,8,192]{2,1,0:T(8,128)S(1)}, f32[8,8,192,128]{3,2,1,0:T(8,128)}) %tuple.107, (s32[]{:T(128)}, s32[1,768]{1,0:T(1,128)S(1)}, ...), branch_computations={%region_1.0_spmd, %region_2.4_spmd} | conditional | flops 4938966016 | bytes 190130080 | solution.py:64
  511.8 2.1 constant_dynamic-slice_fusion.1
  513.9 17.2 %fusion = (f32[8,8,192]{2,1,0:T(8,128)S(1)}, f32[8,768,192,8]{1,2,3,0:T(8,128)}) fusion(pred[192,768]{1,0:T(8,128)(4,1)S(1)} %broadcast_compare_fusion, bf16[768,8,128,1]{0,2,3,1:T(8,128)(2,1)S(1)} %bitcast.483, bf16[192,8,8,128]{3,0,2,1:T(8,128)(2,1)} %get-tuple-element.211), kind=kOutput, calls=%fused_computation.2 | convolution fusion | flops 2444218368 | bytes 42663936 | tf_op jit(solution)/shard_map/while/body/eval_jaxpr/cond/branch_1_fun/tkgd,skd->kgts/dot_general | solution.py:29
  531.0 17.0 %fusion.4 = f32[8,8,192]{2,1,0:T(8,128)S(1)} fusion(f32[8,768,192,8]{1,2,3,0:T(8,128)} %get-tuple-element.276, f32[8,8,192]{2,1,0:T(8,128)S(1)} %max.122, pred[192,768]{1,0:T(8,128)(4,1)S(1)} %broadcast_compare_fusion), kind=kLoop, calls=%fused_computation.6 | loop fusion | flops 37736448 | bytes 37994496 | tf_op jit(solution)/shard_map/while/body/eval_jaxpr/cond/branch_1_fun/reduce_sum | solution.py:36
  548.1 16.7 %multiply_add_fusion = f32[8,8,192,128]{3,2,1,0:T(8,128)S(1)} fusion(f32[8,8,192,128]{3,2,1,0:T(8,128)S(1)} %copy-done, f32[8,8,192]{2,1,0:T(8,128)S(1)} %get-tuple-element.260, bf16[768,8,128,1]{0,2,3,1:T(8,128)(2,1)S(1)} %bitcast.484, f32[8,768,192,8]{1,2,3,0:T(8,128)} %get-tuple-element.276, f32[8,8,192]{2,1,0:T(8,128)S(1)} %max.122, ...), kind=kOutput, calls=%fused_computation.9 | convolution fusion | flops 2456813568 | bytes 52150272 | tf_op jit(solution)/shard_map/while/body/eval_jaxpr/cond/branch_1_fun/kgts,skd->kgtd/dot_general | solution.py:37
  564.9 2.6 copy-done.1
  568.8 56.0 %conditional.2 = ((f32[8,8,192]{2,1,0:T(8,128)S(1)}, f32[8,8,192]{2,1,0:T(8,128)S(1)}, f32[8,8,192,128]{3,2,1,0:T(8,128)})) conditional(s32[]{:T(128)} %convert_element_type.108, (f32[8,8,192]{2,1,0:T(8,128)S(1)}, f32[8,8,192]{2,1,0:T(8,128)S(1)}, f32[8,8,192,128]{3,2,1,0:T(8,128)}) %tuple.107, (s32[]{:T(128)}, s32[1,768]{1,0:T(1,128)S(1)}, ...), branch_computations={%region_1.0_spmd, %region_2.4_spmd} | conditional | flops 4938966016 | bytes 190130080 | solution.py:64
  569.0 2.2 constant_dynamic-slice_fusion.1
  571.2 17.2 %fusion = (f32[8,8,192]{2,1,0:T(8,128)S(1)}, f32[8,768,192,8]{1,2,3,0:T(8,128)}) fusion(pred[192,768]{1,0:T(8,128)(4,1)S(1)} %broadcast_compare_fusion, bf16[768,8,128,1]{0,2,3,1:T(8,128)(2,1)S(1)} %bitcast.483, bf16[192,8,8,128]{3,0,2,1:T(8,128)(2,1)} %get-tuple-element.211), kind=kOutput, calls=%fused_computation.2 | convolution fusion | flops 2444218368 | bytes 42663936 | tf_op jit(solution)/shard_map/while/body/eval_jaxpr/cond/branch_1_fun/tkgd,skd->kgts/dot_general | solution.py:29
  588.4 17.0 %fusion.4 = f32[8,8,192]{2,1,0:T(8,128)S(1)} fusion(f32[8,768,192,8]{1,2,3,0:T(8,128)} %get-tuple-element.276, f32[8,8,192]{2,1,0:T(8,128)S(1)} %max.122, pred[192,768]{1,0:T(8,128)(4,1)S(1)} %broadcast_compare_fusion), kind=kLoop, calls=%fused_computation.6 | loop fusion | flops 37736448 | bytes 37994496 | tf_op jit(solution)/shard_map/while/body/eval_jaxpr/cond/branch_1_fun/reduce_sum | solution.py:36
  605.5 16.7 %multiply_add_fusion = f32[8,8,192,128]{3,2,1,0:T(8,128)S(1)} fusion(f32[8,8,192,128]{3,2,1,0:T(8,128)S(1)} %copy-done, f32[8,8,192]{2,1,0:T(8,128)S(1)} %get-tuple-element.260, bf16[768,8,128,1]{0,2,3,1:T(8,128)(2,1)S(1)} %bitcast.484, f32[8,768,192,8]{1,2,3,0:T(8,128)} %get-tuple-element.276, f32[8,8,192]{2,1,0:T(8,128)S(1)} %max.122, ...), kind=kOutput, calls=%fused_computation.9 | convolution fusion | flops 2456813568 | bytes 52150272 | tf_op jit(solution)/shard_map/while/body/eval_jaxpr/cond/branch_1_fun/kgts,skd->kgtd/dot_general | solution.py:37
  622.2 2.6 copy-done.1
  624.8 4.7 fusion.12
  629.5 2.0 copy.72
  631.6 4.5 copy.316
  (154 shorter events, 42.8 us)
Async XLA Ops:
  7.2 95.0 %all-gather.2.cloned.1.call-start = ((), (), s32[]{:S(2)}) async-start(), calls=%async_computation | async-start | bytes 25952256 | tf_op jit(solution)/shard_map/all_gather | solution.py:114
  12.8 3.9 copy-start.2
  16.6 0.6 copy-start.5
  17.1 1.2 copy-start.3
  18.3 0.7 copy-start.4
  18.4 0.8 slice-start
  187.3 17.1 %copy-start = (f32[8,8,192,128]{3,2,1,0:T(8,128)S(1)}, f32[8,8,192,128]{3,2,1,0:T(8,128)}, u32[]{:S(2)}) copy-start(f32[8,8,192,128]{3,2,1,0:T(8,128)} %get-tuple-element.213) | copy-start | bytes 18874372 | tf_op jit(solution)/shard_map/while/body/eval_jaxpr/cond
  221.2 2.6 copy-start.1
  244.6 17.1 %copy-start = (f32[8,8,192,128]{3,2,1,0:T(8,128)S(1)}, f32[8,8,192,128]{3,2,1,0:T(8,128)}, u32[]{:S(2)}) copy-start(f32[8,8,192,128]{3,2,1,0:T(8,128)} %get-tuple-element.213) | copy-start | bytes 18874372 | tf_op jit(solution)/shard_map/while/body/eval_jaxpr/cond
  278.4 2.6 copy-start.1
  301.9 17.1 %copy-start = (f32[8,8,192,128]{3,2,1,0:T(8,128)S(1)}, f32[8,8,192,128]{3,2,1,0:T(8,128)}, u32[]{:S(2)}) copy-start(f32[8,8,192,128]{3,2,1,0:T(8,128)} %get-tuple-element.213) | copy-start | bytes 18874372 | tf_op jit(solution)/shard_map/while/body/eval_jaxpr/cond
  335.7 2.6 copy-start.1
  359.2 17.1 %copy-start = (f32[8,8,192,128]{3,2,1,0:T(8,128)S(1)}, f32[8,8,192,128]{3,2,1,0:T(8,128)}, u32[]{:S(2)}) copy-start(f32[8,8,192,128]{3,2,1,0:T(8,128)} %get-tuple-element.213) | copy-start | bytes 18874372 | tf_op jit(solution)/shard_map/while/body/eval_jaxpr/cond
  393.0 2.6 copy-start.1
  416.5 17.1 %copy-start = (f32[8,8,192,128]{3,2,1,0:T(8,128)S(1)}, f32[8,8,192,128]{3,2,1,0:T(8,128)}, u32[]{:S(2)}) copy-start(f32[8,8,192,128]{3,2,1,0:T(8,128)} %get-tuple-element.213) | copy-start | bytes 18874372 | tf_op jit(solution)/shard_map/while/body/eval_jaxpr/cond
  450.3 2.6 copy-start.1
  473.7 17.1 %copy-start = (f32[8,8,192,128]{3,2,1,0:T(8,128)S(1)}, f32[8,8,192,128]{3,2,1,0:T(8,128)}, u32[]{:S(2)}) copy-start(f32[8,8,192,128]{3,2,1,0:T(8,128)} %get-tuple-element.213) | copy-start | bytes 18874372 | tf_op jit(solution)/shard_map/while/body/eval_jaxpr/cond
  507.6 2.6 copy-start.1
  531.0 17.1 %copy-start = (f32[8,8,192,128]{3,2,1,0:T(8,128)S(1)}, f32[8,8,192,128]{3,2,1,0:T(8,128)}, u32[]{:S(2)}) copy-start(f32[8,8,192,128]{3,2,1,0:T(8,128)} %get-tuple-element.213) | copy-start | bytes 18874372 | tf_op jit(solution)/shard_map/while/body/eval_jaxpr/cond
  564.9 2.6 copy-start.1
  588.4 17.1 %copy-start = (f32[8,8,192,128]{3,2,1,0:T(8,128)S(1)}, f32[8,8,192,128]{3,2,1,0:T(8,128)}, u32[]{:S(2)}) copy-start(f32[8,8,192,128]{3,2,1,0:T(8,128)} %get-tuple-element.213) | copy-start | bytes 18874372 | tf_op jit(solution)/shard_map/while/body/eval_jaxpr/cond
  622.2 2.6 copy-start.1
Sparse Core Ops, SparseCore 0:
  10.2 91.8 all-gather.1
where the time goes:
time: 656 us; the launch traced here: 643 us
  matrix products  302 us (46%)
  other arithmetic  153 us (23%)
  local copies, waits for them, and re-layouts  133 us (20%)
  waiting for transfers between devices  33.4 us (5%)
  between operations  14.9 us (2%)
  loops' own time  6.58 us (1%)
    dot_general x18, matrix products, update_state(): jnp.einsum('tkgd,skd->kgts', query_rows, key_part, preferred_element_type...  153 us
    dot_general x18, matrix products, update_state(): jnp.einsum('kgts,skd->kgtd', weights.astype(jnp.bfloat16), value_part, pr...  149 us
    reduce_sum x13, other arithmetic, update_state(): totals = totals * factor + jnp.sum(weights, axis=-1)  143 us
    while x2, local copies, waits for them, and re-layouts, fold_step(): return lax.fori_loop(0, turns, one_turn, running)  64.4 us
    all_gather x1, waiting for transfers between devices, on_device(): gathered = lax.all_gather(long_kv, ('ctx', 'head'), axis=1, tiled=True)  33.4 us
    cond x40, local copies, waits for them, and re-layouts  21 us
    unnamed x29, local copies, waits for them, and re-layouts  17 us
    slice x8, local copies, waits for them, and re-layouts, update_state(): stacked_rows[1].reshape(stacked_rows.shape[1], kv_heads, head_dim)  16.9 us
  transfers between devices with their start and end apart: 1, of which 1 were waited for; matrix products, arithmetic and copies ran while one was open for 9% of the time, Pallas kernels for 0%

commit v1 on v0

v1 whole, which is shorter than its diff:
```python
import functools
import math

import jax
import jax.numpy as jnp
from jax import lax
from jax.experimental import pallas as pl
from jax.experimental.pallas import tpu as pltpu
from jax.sharding import PartitionSpec as P

QUERY_HEAD_COUNT = 64
KEY_VALUE_HEADS = 8
HEAD_SIZE = 128
GROUP = QUERY_HEAD_COUNT // KEY_VALUE_HEADS

NEG_LARGE = -1e30
LOG2_SCALE = math.log2(math.e) / math.sqrt(HEAD_SIZE)
PIECE_HEADS = 2
KEY_BLOCK = 1536


def dot_nt(a, b):
    return lax.dot_general(a, b, (((1,), (1,)), ((), ())), preferred_element_type=jnp.float32)


def long_kernel(q_ref, k_ref, v_ref, held_ref, o_ref, acc, high, total, *, rows, block):
    shards, tokens = k_ref.shape[0], k_ref.shape[1]
    per_block = block // tokens
    rank = lax.axis_index("ctx") * lax.axis_size("head") + lax.axis_index("head")
    full = rank // per_block
    acc[...] = jnp.zeros_like(acc)
    total[...] = jnp.zeros_like(total)
    high[...] = jnp.full_like(high, NEG_LARGE)

    def one_block(index, masked):
        shard = pl.multiple_of(index * per_block, per_block)
        k = k_ref[pl.ds(shard, per_block)].reshape(block, HEAD_SIZE)
        v = v_ref[pl.ds(shard, per_block)].reshape(block, HEAD_SIZE)
        v_one = jnp.concatenate([v, jnp.ones_like(v)], axis=1)
        if masked:
            q_pos = (rank - shard) * tokens + lax.broadcasted_iota(jnp.int32, (rows, block), 0)
            allowed = lax.broadcasted_iota(jnp.int32, (rows, block), 1) <= q_pos
        for h in range(GROUP):
            r = slice(h * rows, (h + 1) * rows)
            s = dot_nt(q_ref[:, h * HEAD_SIZE : (h + 1) * HEAD_SIZE], k)
            if masked:
                s = jnp.where(allowed, s, NEG_LARGE)
            old = high[r, :]
            new = jnp.maximum(old, jnp.max(s, axis=1, keepdims=True) * LOG2_SCALE)
            factor = jnp.exp2(old - new)
            p = jnp.exp2(s * LOG2_SCALE - new[:, :1]).astype(jnp.bfloat16)
            mixed = jnp.dot(p, v_one, preferred_element_type=jnp.float32)
            high[r, :] = new
            acc[r, :] = acc[r, :] * factor + mixed[:, :HEAD_SIZE]
            total[r, :] = total[r, :] * factor + mixed[:, HEAD_SIZE:]

    def body(index, carry):
        one_block(index, False)
        return carry

    lax.fori_loop(0, full, body, 0)
    one_block(full, True)
    for h in range(GROUP):
        r = slice(h * rows, (h + 1) * rows)
        o_ref[:, h * HEAD_SIZE : (h + 1) * HEAD_SIZE] = (acc[r, :] / total[r, :]).astype(o_ref.dtype)


def long_piece(query, gathered, held, piece):
    rows = query.shape[0]
    shards, _, tokens, width = gathered.shape
    heads = width // HEAD_SIZE
    first = piece * heads
    wide = GROUP * HEAD_SIZE
    flops = heads * GROUP * rows * shards * tokens * HEAD_SIZE * 4
    args = [query, gathered, gathered]
    in_specs = [
        pl.BlockSpec((rows, wide), lambda g: (0, first + g)),
        pl.BlockSpec((shards, None, tokens, HEAD_SIZE), lambda g: (0, 0, 0, g)),
        pl.BlockSpec((shards, None, tokens, HEAD_SIZE), lambda g: (0, 1, 0, g)),
    ]
    kernel = functools.partial(long_kernel, rows=rows, block=KEY_BLOCK)
    aliases = {}
    if held is None:
        body = lambda q, k, v, o, *rest: kernel(q, k, v, None, o, *rest)
    else:
        body = kernel
        args.append(held)
        in_specs.append(pl.BlockSpec(memory_space=pl.ANY))
        aliases = {3: 0}
    return pl.pallas_call(
        body,
        out_shape=jax.ShapeDtypeStruct(query.shape, query.dtype),
        grid=(heads,),
        in_specs=in_specs,
        out_specs=pl.BlockSpec((rows, wide), lambda g: (0, first + g)),
        scratch_shapes=[pltpu.VMEM((GROUP * rows, HEAD_SIZE), jnp.float32)] * 3,
        input_output_aliases=aliases,
        compiler_params=pltpu.CompilerParams(vmem_limit_bytes=50 << 20),
        cost_estimate=pl.CostEstimate(flops=flops, bytes_accessed=8 << 20, transcendentals=flops // 512),
        name=f"long_piece_{piece}",
    )(*args)


def short_kernel(q_ref, k_ref, v_ref, seg_row_ref, seg_col_ref, o_ref):
    tokens = q_ref.shape[0]
    half = tokens // 2
    k, v = k_ref[...], v_ref[...]
    v_one = jnp.concatenate([v, jnp.ones_like(v)], axis=1)
    labels_q = seg_col_ref[...]
    labels_k = seg_row_ref[...]
    for part in range(2):
        low, keys = part * half, (part + 1) * half
        q_pos = low + lax.broadcasted_iota(jnp.int32, (half, keys), 0)
        k_pos = lax.broadcasted_iota(jnp.int32, (half, keys), 1)
        same = labels_q[low : low + half, :1] == labels_k[:1, :keys]
        allowed = (k_pos <= q_pos) & same
        for h in range(GROUP):
            c = slice(h * HEAD_SIZE, (h + 1) * HEAD_SIZE)
            s = dot_nt(q_ref[low : low + half, c], k[:keys])
            s = jnp.where(allowed, s, NEG_LARGE)
            top = jnp.max(s, axis=1, keepdims=True)
            p = jnp.exp2((s - top) * LOG2_SCALE).astype(jnp.bfloat16)
            mixed = jnp.dot(p, v_one[:keys], preferred_element_type=jnp.float32)
            o_ref[low : low + half, c] = (mixed[:, :HEAD_SIZE] / mixed[:, HEAD_SIZE:]).astype(o_ref.dtype)


def attend_short(query, key_value, seg):
    tokens = query.shape[0]
    wide = GROUP * HEAD_SIZE
    seg_row = jnp.broadcast_to(seg, (8, tokens))
    seg_col = jnp.broadcast_to(seg.reshape(tokens, 1), (tokens, HEAD_SIZE))
    flops = QUERY_HEAD_COUNT * tokens * tokens * HEAD_SIZE * 4
    return pl.pallas_call(
        short_kernel,
        out_shape=jax.ShapeDtypeStruct(query.shape, query.dtype),
        grid=(KEY_VALUE_HEADS,),
        in_specs=[
            pl.BlockSpec((tokens, wide), lambda g: (0, g)),
            pl.BlockSpec((None, tokens, HEAD_SIZE), lambda g: (0, 0, g)),
            pl.BlockSpec((None, tokens, HEAD_SIZE), lambda g: (1, 0, g)),
            pl.BlockSpec((8, tokens), lambda g: (0, 0)),
            pl.BlockSpec((tokens, HEAD_SIZE), lambda g: (0, 0)),
        ],
        out_specs=pl.BlockSpec((tokens, wide), lambda g: (0, g)),
        cost_estimate=pl.CostEstimate(flops=flops, bytes_accessed=9 << 20, transcendentals=flops // 512),
        name="short_docs",
    )(query, key_value, key_value, seg_row, seg_col)


def on_device(long_query, long_kv, short_query, short_key_value, short_seg):
    width = PIECE_HEADS * HEAD_SIZE
    gathered = []
    for piece in range(KEY_VALUE_HEADS // PIECE_HEADS):
        part = long_kv[:, :, piece * width : (piece + 1) * width]
        gathered.append(lax.all_gather(part, ("ctx", "head"), axis=0, tiled=False))
    short_out = attend_short(short_query, short_key_value, short_seg)
    long_out = None
    for piece, part in enumerate(gathered):
        long_out = long_piece(long_query, part, long_out, piece)
    return (long_out, short_out)


def solution(mesh):
    return jax.shard_map(
        on_device,
        mesh=mesh,
        in_specs=(
            P(("dp", "ctx", "head"), None),
            P(None, ("dp", "ctx", "head"), None),
            P(("dp", "ctx", "head"), None),
            P(None, ("dp", "ctx", "head"), None),
            P(("dp", "ctx", "head"), None),
        ),
        out_specs=(P(("dp", "ctx", "head"), None), P(("dp", "ctx", "head"), None)),
        check_vma=False,
    )
```

time: 656 us -> 250 us (0.38)
  the two profiles are of different devices: /device:TPU:89 before, /device:TPU:25 now
where the time goes in v1:
time: 250 us
  Pallas kernels  149 us (60%)
  waiting for transfers between devices  82.3 us (33%)
  between operations  13.8 us (6%)
  local copies, waits for them, and re-layouts  4.83 us (2%)
    pallas_call x4, Pallas kernels, long_piece(): pl.pallas_call(body, out_shape=jax.ShapeDtypeStruct(query.shape, query.dt...  126 us
    all_gather x4, waiting for transfers between devices, on_device(): gathered.append(lax.all_gather(part, ('ctx', 'head'), axis=0, tiled=False))  80.3 us
    pallas_call x1, Pallas kernels, attend_short(): pl.pallas_call(short_kernel, out_shape=jax.ShapeDtypeStruct(query.shape,...  22.5 us
  transfers between devices with their start and end apart: 4, of which 4 were waited for; matrix products, arithmetic and copies ran while one was open for 1% of the time, Pallas kernels for 47%

profile of v1, /device:TPU:25, one launch (start us, length us, event | category | flops | bytes accessed | tf_op | source)
XLA Modules:
  0.0 249.8 jit_solution(8533264564360245417)
XLA Ops:
  7.2 0.0 all-gather.15.cloned.1.call-start
  7.2 2.1 fusion
  9.3 0.0 all-gather.15.cloned.1.call-update
  9.4 0.0 all-gather.13.cloned.1.call-start
  9.4 0.7 all-gather.13.cloned.1.call-update
  10.1 0.0 all-gather.11.cloned.1.call-start
  10.2 0.7 all-gather.11.cloned.1.call-update
  10.8 0.0 all-gather.9.cloned.1.call-start
  10.9 0.5 all-gather.9.cloned.1.call-update
  11.4 1.4 broadcast_in_dim.14.seg_col_ref
  12.8 1.3 broadcast_in_dim.13.seg_row_ref
  14.1 0.0 copy-start
  14.1 22.5 %short_docs.1 = bf16[256,8192]{1,0:T(8,128)(2,1)} custom-call(bf16[256,8192]{1,0:T(8,128)(2,1)} %q_ref.7, bf16[2,256,1024]{2,1,0:T(8,128)(2,1)} %v_ref.1, bf16[2,256,1024]{2,1,0:T(8,128)(2,1)} %v_ref.1, s32[8,256]{1,0:T(8,128)} %broadcast_in_dim.13.seg_row_ref, s32[256,128]{1,0:T(8,128)} %broadcast_in_dim.14.seg_col_ref), custom_call_target="tpu_custom_call" | custom-call | flops 2147483648 | bytes 9437184 | tf_op jit(solution)/shard_map/short_docs/pallas_call | solution.py:133
  36.6 24.9 %all-gather.15.cloned.1.call-done = bf16[64,192,256]{2,1,0:T(8,128)(2,1)} async-done(((bf16[2,192,256]{2,1,0:T(8,128)(2,1)}), bf16[64,192,256]{2,1,0:T(8,128)(2,1)}) %all-gather.15.cloned.1.call-update) | async-done | bytes 6291472 | tf_op jit(solution)/shard_map/all_gather | solution.py:155
  61.5 0.0 copy-done
  61.5 31.6 %long_piece_0.1.held_ref = bf16[192,8192]{1,0:T(8,128)(2,1)} custom-call(bf16[192,8192]{1,0:T(8,128)(2,1)S(1)} %copy-done, bf16[32,2,192,256]{3,2,1,0:T(8,128)(2,1)} %bitcast.7, bf16[32,2,192,256]{3,2,1,0:T(8,128)(2,1)} %bitcast.8), custom_call_target="tpu_custom_call" | custom-call | flops 9663676416 | bytes 8388608 | tf_op jit(solution)/shard_map/long_piece_0/pallas_call | solution.py:90
  93.1 18.5 %all-gather.13.cloned.1.call-done = bf16[64,192,256]{2,1,0:T(8,128)(2,1)} async-done(((bf16[2,192,256]{2,1,0:T(8,128)(2,1)}), bf16[64,192,256]{2,1,0:T(8,128)(2,1)}) %all-gather.13.cloned.1.call-update) | async-done | bytes 6291472 | tf_op jit(solution)/shard_map/all_gather | solution.py:155
  111.6 31.6 %long_piece_1.1.held_ref = bf16[192,8192]{1,0:T(8,128)(2,1)} custom-call(bf16[192,8192]{1,0:T(8,128)(2,1)S(1)} %copy-done, bf16[32,2,192,256]{3,2,1,0:T(8,128)(2,1)} %bitcast.9, bf16[32,2,192,256]{3,2,1,0:T(8,128)(2,1)} %bitcast.10, bf16[192,8192]{1,0:T(8,128)(2,1)} %long_piece_0.1.held_ref), custom_call_target="tpu_custom_call", output_to_operand_aliasing={{}: (3, {})} | custom-call | flops 9663676416 | bytes 8388608 | tf_op jit(solution)/shard_map/long_piece_1/pallas_call | solution.py:90
  143.2 18.5 %all-gather.11.cloned.1.call-done = bf16[64,192,256]{2,1,0:T(8,128)(2,1)} async-done(((bf16[2,192,256]{2,1,0:T(8,128)(2,1)}), bf16[64,192,256]{2,1,0:T(8,128)(2,1)}) %all-gather.11.cloned.1.call-update) | async-done | bytes 6291472 | tf_op jit(solution)/shard_map/all_gather | solution.py:155
  161.7 31.6 %long_piece_2.1.held_ref = bf16[192,8192]{1,0:T(8,128)(2,1)} custom-call(bf16[192,8192]{1,0:T(8,128)(2,1)S(1)} %copy-done, bf16[32,2,192,256]{3,2,1,0:T(8,128)(2,1)} %bitcast.11, bf16[32,2,192,256]{3,2,1,0:T(8,128)(2,1)} %bitcast.12, bf16[192,8192]{1,0:T(8,128)(2,1)} %long_piece_1.1.held_ref), custom_call_target="tpu_custom_call", output_to_operand_aliasing={{}: (3, {})} | custom-call | flops 9663676416 | bytes 8388608 | tf_op jit(solution)/shard_map/long_piece_2/pallas_call | solution.py:90
  193.3 18.4 %all-gather.9.cloned.1.call-done = bf16[64,192,256]{2,1,0:T(8,128)(2,1)} async-done(((bf16[2,192,256]{2,1,0:T(8,128)(2,1)}), bf16[64,192,256]{2,1,0:T(8,128)(2,1)}) %all-gather.9.cloned.1.call-update) | async-done | bytes 6291472 | tf_op jit(solution)/shard_map/all_gather | solution.py:155
  211.6 31.6 %long_piece_3.1 = bf16[192,8192]{1,0:T(8,128)(2,1)} custom-call(bf16[192,8192]{1,0:T(8,128)(2,1)S(1)} %copy-done, bf16[32,2,192,256]{3,2,1,0:T(8,128)(2,1)} %bitcast.13, bf16[32,2,192,256]{3,2,1,0:T(8,128)(2,1)} %bitcast.14, bf16[192,8192]{1,0:T(8,128)(2,1)} %long_piece_2.1.held_ref), custom_call_target="tpu_custom_call", output_to_operand_aliasing={{}: (3, {})} | custom-call | flops 9663676416 | bytes 8388608 | tf_op jit(solution)/shard_map/long_piece_3/pallas_call | solution.py:90
Async XLA Ops:
  7.2 54.3 %all-gather.15.cloned.1.call-start = ((), (), s32[]{:S(2)}) async-start(), calls=%async_computation.3 | async-start | bytes 6488064 | tf_op jit(solution)/shard_map/all_gather | solution.py:155
  9.4 102.2 %all-gather.13.cloned.1.call-start = ((), (), s32[]{:S(2)}) async-start(), calls=%async_computation.2 | async-start | bytes 6488064 | tf_op jit(solution)/shard_map/all_gather | solution.py:155
  10.1 151.6 %all-gather.11.cloned.1.call-start = ((), (), s32[]{:S(2)}) async-start(), calls=%async_computation.1 | async-start | bytes 6488064 | tf_op jit(solution)/shard_map/all_gather | solution.py:155
  10.8 200.8 %all-gather.9.cloned.1.call-start = ((), (), s32[]{:S(2)}) async-start(), calls=%async_computation | async-start | bytes 6488064 | tf_op jit(solution)/shard_map/all_gather | solution.py:155
  14.1 47.4 %copy-start = (bf16[192,8192]{1,0:T(8,128)(2,1)S(1)}, bf16[192,8192]{1,0:T(8,128)(2,1)}, u32[]{:S(2)}) copy-start(bf16[192,8192]{1,0:T(8,128)(2,1)} %q_ref.6) | copy-start | bytes 9437188
Sparse Core Ops, SparseCore 0:
  10.8 50.6 all-gather.14
  63.8 47.7 all-gather.12
  113.9 47.7 all-gather.10
  163.8 47.7 all-gather.8

commit v2 on v0

v2 whole, which is shorter than its diff:
```python
import functools
import math

import jax
import jax.numpy as jnp
from jax import lax
from jax.experimental import pallas as pl
from jax.experimental.pallas import tpu as pltpu
from jax.sharding import PartitionSpec as P

QUERY_HEAD_COUNT = 64
KEY_VALUE_HEADS = 8
HEAD_SIZE = 128
GROUP = QUERY_HEAD_COUNT // KEY_VALUE_HEADS
WIDE = GROUP * HEAD_SIZE

NEG_LARGE = -1e30
LOG2_SCALE = math.log2(math.e) / math.sqrt(HEAD_SIZE)

SIDE = 4
LOCAL_HEADS = KEY_VALUE_HEADS // 2
PAIR = LOCAL_HEADS // 2
PAIR_WIDTH = PAIR * HEAD_SIZE
MESH = pl.DeviceIdType.MESH

NEAR, FAR, RESULT, COPIES = 3, 11, 43, 45


def dot_nt(a, b):
    return lax.dot_general(a, b, (((1,), (1,)), ((), ())), preferred_element_type=jnp.float32)


def wrap(x):
    return lax.rem(x + SIDE, SIDE)


def order_of(index, half, core):
    return jnp.where(index < half, core * half + index, (1 - core) * half + index - half)


def kernel(
    q_hbm, kv_hbm, short_q_hbm, short_kv_hbm, seg_row, seg_col, out_hbm, short_out_hbm,
    q, kv, acc, high, total, score_0, score_1, result, short_q, short_kv, send, recv, local,
):
    half = q_hbm.shape[0]
    rows = 2 * half
    ctx, head = lax.axis_index("ctx"), lax.axis_index("head")
    y, z, core = lax.div(ctx, 2), lax.rem(ctx, 2) * 2 + lax.div(head, 2), lax.rem(head, 2)
    chip = y * SIDE + z
    q_columns = LOCAL_HEADS * WIDE

    def device(to_y, to_z, to_core):
        return {"ctx": to_y * 2 + lax.div(to_z, 2), "head": lax.rem(to_z, 2) * 2 + to_core}

    mate = device(y, z, 1 - core)
    ahead = (device(y, wrap(z + 1), core), device(wrap(y + 1), z, core))
    behind = (device(y, wrap(z - 1), core), device(wrap(y - 1), z, core))

    def remote(src, dst, index, target):
        return pltpu.make_async_remote_copy(
            src_ref=src, dst_ref=dst, send_sem=send.at[index], recv_sem=recv.at[index], device_id=target, device_id_type=MESH
        )

    def mine_columns(side, of_core):
        start = of_core * (LOCAL_HEADS * HEAD_SIZE) + side * PAIR_WIDTH
        return pl.ds(pl.multiple_of(start, PAIR_WIDTH), PAIR_WIDTH)

    def heads_of(of_core, start, size):
        return pl.ds(pl.multiple_of(of_core * q_columns + start, size), size)

    def mate_kv(side):
        return remote(kv_hbm.at[:, :, mine_columns(side, 1 - core)], kv.at[side, 0, :, 0, pl.ds(half, half)], 1 + side, mate)

    def mate_q():
        return remote(q_hbm.at[:, heads_of(1 - core, 0, q_columns)], q.at[1], 0, mate)

    def near(side, which):
        index = NEAR + 4 * side + which
        if which == 0:
            return remote(kv.at[side, 0, :, 0], kv.at[side, 0, :, 1], index, ahead[side])
        if which == 1:
            return remote(kv.at[side, 0, :, 0], kv.at[side, 0, :, 2], index, behind[side])
        if which == 2:
            return remote(kv.at[side, 0, 0, 1], kv.at[side, 0, 0, 3], index, ahead[side])
        return remote(kv.at[side, 0, 1, 2], kv.at[side, 0, 1, 3], index, behind[side])

    def far(side, piece, which):
        index = FAR + 16 * side + 4 * piece + which
        unit, slot = 1 + piece // 2, 2 * (piece % 2)
        if which == 0:
            return remote(kv.at[side, 0, :, piece], kv.at[side, unit, :, slot], index, ahead[1 - side])
        if which == 1:
            return remote(kv.at[side, 0, :, piece], kv.at[side, unit, :, slot + 1], index, behind[1 - side])
        if which == 2:
            return remote(kv.at[side, unit, 0, slot], kv.at[side, 3, 0, piece], index, ahead[1 - side])
        return remote(kv.at[side, unit, 1, slot + 1], kv.at[side, 3, 1, piece], index, behind[1 - side])

    def give_back(side):
        columns = heads_of(core, side * (PAIR * WIDE), PAIR * WIDE)
        return remote(result.at[1, side], out_hbm.at[:, columns], RESULT + side, mate)

    def keep(side):
        columns = heads_of(core, side * (PAIR * WIDE), PAIR * WIDE)
        return pltpu.make_async_copy(result.at[0, side], out_hbm.at[:, columns], local.at[5 + side])

    own_q = pltpu.make_async_copy(q_hbm.at[:, heads_of(core, 0, q_columns)], q.at[0], local.at[0])
    own_kv = [
        pltpu.make_async_copy(kv_hbm.at[:, :, mine_columns(side, core)], kv.at[side, 0, :, 0, pl.ds(0, half)], local.at[1 + side])
        for side in range(2)
    ]
    get_short_q = pltpu.make_async_copy(short_q_hbm, short_q, local.at[3])
    get_short_kv = pltpu.make_async_copy(short_kv_hbm, short_kv, local.at[4])
    put_short = pltpu.make_async_copy(short_q, short_out_hbm, local.at[7])

    own_kv[0].start()
    own_kv[1].start()
    barrier = pltpu.get_barrier_semaphore()
    for target in (mate,) + ahead + behind:
        pl.semaphore_signal(barrier, inc=1, device_id=target, device_id_type=MESH)
    pl.semaphore_wait(barrier, 5)
    for side in range(2):
        mate_kv(side).start()
    mate_q().start()
    get_short_kv.start()
    get_short_q.start()
    own_q.start()
    for side in range(2):
        own_kv[side].wait()
        mate_kv(side).wait_recv()
        near(side, 0).start()
        near(side, 1).start()
    for side in range(2):
        far(side, 0, 0).start()
        far(side, 0, 1).start()

    tokens = short_q.shape[0]
    part_rows = tokens // 2

    def short_head(g, carry):
        key_columns = pl.ds(pl.multiple_of(g * HEAD_SIZE, HEAD_SIZE), HEAD_SIZE)
        k, v = short_kv[0, :, key_columns], short_kv[1, :, key_columns]
        v_one = jnp.concatenate([v, jnp.ones_like(v)], axis=1)
        columns = [pl.ds(pl.multiple_of(g * WIDE + h * HEAD_SIZE, HEAD_SIZE), HEAD_SIZE) for h in range(GROUP)]
        for part in range(2):
            low, keys = part * part_rows, (part + 1) * part_rows
            q_pos = low + lax.broadcasted_iota(jnp.int32, (part_rows, keys), 0)
            k_pos = lax.broadcasted_iota(jnp.int32, (part_rows, keys), 1)
            same = seg_col[low : low + part_rows, :1] == seg_row[:1, :keys]
            allowed = (k_pos <= q_pos) & same
            weights = []
            for s in [dot_nt(short_q[low : low + part_rows, c], k[:keys]) for c in columns]:
                s = jnp.where(allowed, s, NEG_LARGE)
                top = jnp.max(s, axis=1, keepdims=True)
                weights.append(jnp.exp2((s - top) * LOG2_SCALE).astype(jnp.bfloat16))
            mixes = [jnp.dot(p, v_one[:keys], preferred_element_type=jnp.float32) for p in weights]
            for c, mixed in zip(columns, mixes):
                short_q[low : low + part_rows, c] = (mixed[:, :HEAD_SIZE] / mixed[:, HEAD_SIZE:]).astype(jnp.bfloat16)
        return carry

    get_short_kv.wait()
    get_short_q.wait()

    def short_step(g, carry):
        short_head(g, carry)

        @pl.when(g == 5)
        def _():
            for side in range(2):
                near(side, 0).wait_recv()
                near(side, 2).start()
                near(side, 1).wait_recv()
                near(side, 3).start()
            for piece in (1, 2):
                for side in range(2):
                    far(side, piece, 0).start()
                    far(side, piece, 1).start()

        return carry

    lax.fori_loop(0, KEY_VALUE_HEADS, short_step, 0)
    put_short.start()
    own_q.wait()
    mate_q().wait_recv()
    for side in range(2):
        near(side, 2).wait_recv()
        near(side, 3).wait_recv()
        far(side, 3, 0).start()
        far(side, 3, 1).start()

    q_pos = chip * rows + order_of(lax.broadcasted_iota(jnp.int32, (rows, 1), 0), half, core)
    key_index = order_of(lax.broadcasted_iota(jnp.int32, (1, rows), 1), half, core)

    def phase(number, carry):
        unit, side = lax.div(number, 2), lax.rem(number, 2)
        owners = []
        for slot in range(SIDE):
            beyond = lax.div(slot, 2) + 2 * (unit - 1)
            ring = jnp.where(jnp.logical_or(unit == 0, unit == 3), slot, beyond)
            along = jnp.where(ring == 1, -1, jnp.where(ring == 2, 1, jnp.where(ring == 3, 2, 0)))
            across = jnp.where(unit == 0, 0, jnp.where(unit == 3, 2, 2 * (slot % 2) - 1))
            owner_y = wrap(y + jnp.where(side == 0, across, along))
            owner_z = wrap(z + jnp.where(side == 0, along, across))
            owners.append(owner_y * SIDE + owner_z)
        low = jnp.minimum(jnp.minimum(owners[0], owners[1]), jnp.minimum(owners[2], owners[3]))
        top = jnp.maximum(jnp.maximum(owners[0], owners[1]), jnp.maximum(owners[2], owners[3]))

        def block(local_head, plane):
            columns = pl.ds(pl.multiple_of(local_head * HEAD_SIZE, HEAD_SIZE), HEAD_SIZE)
            return kv[side, unit, plane, :, :, columns].reshape(SIDE * rows, HEAD_SIZE)

        def scores(item):
            columns = pl.ds(pl.multiple_of((side * PAIR * GROUP + item) * HEAD_SIZE, HEAD_SIZE), HEAD_SIZE)
            query = jnp.concatenate([q[0, :, columns], q[1, :, columns]], axis=0)
            return dot_nt(query, block(lax.div(item, GROUP), 0))

        def update(item, score, masked, first):
            v = block(lax.div(item, GROUP), 1)
            v_one = jnp.concatenate([v, jnp.ones_like(v)], axis=1)
            s = score[...]
            if masked:
                k_pos = jnp.concatenate([owner * rows + key_index for owner in owners], axis=1)
                s = jnp.where(k_pos <= q_pos, s, NEG_LARGE)
            r = pl.ds(pl.multiple_of((side * PAIR * GROUP + item) * rows, rows), rows)
            best = jnp.max(s, axis=1, keepdims=True) * LOG2_SCALE
            if first:
                new = jnp.broadcast_to(best, (rows, HEAD_SIZE))
            else:
                old = high[r, :]
                new = jnp.maximum(old, best)
                factor = jnp.exp2(old - new)
            p = jnp.exp2(s * LOG2_SCALE - new[:, :1]).astype(jnp.bfloat16)
            mixed = jnp.dot(p, v_one, preferred_element_type=jnp.float32)
            high[r, :] = new
            if first:
                acc[r, :] = mixed[:, :HEAD_SIZE]
                total[r, :] = mixed[:, HEAD_SIZE:]
            else:
                acc[r, :] = acc[r, :] * factor + mixed[:, :HEAD_SIZE]
                total[r, :] = total[r, :] * factor + mixed[:, HEAD_SIZE:]

        def run(masked, first):
            items = PAIR * GROUP
            score_0[...] = scores(0)

            def two(couple, inner):
                item = couple * 2
                score_1[...] = scores(item + 1)
                update(item, score_0, masked, first)
                score_0[...] = scores(jnp.minimum(item + 2, items - 1))
                update(item + 1, score_1, masked, first)
                return inner

            lax.fori_loop(0, items // 2, two, 0)

        @pl.when(unit == 0)
        def _():
            run(True, True)

        used = jnp.logical_and(unit > 0, low <= chip)

        @pl.when(jnp.logical_and(used, top < chip))
        def _():
            run(False, False)

        @pl.when(jnp.logical_and(used, top >= chip))
        def _():
            run(True, False)

        def pass_on(pieces):
            for piece in pieces:
                for side in range(2):
                    far(side, piece, 0).wait_recv()
                    far(side, piece, 2).start()
                    far(side, piece, 1).wait_recv()
                    far(side, piece, 3).start()

        @pl.when(number == 0)
        def _():
            pass_on((0,))

        @pl.when(number == 1)
        def _():
            pass_on((1,))

        @pl.when(number == 3)
        def _():
            pass_on((2, 3))

        @pl.when(number == 5)
        def _():
            for piece in range(SIDE):
                for side in range(2):
                    far(side, piece, 2).wait_recv()
                    far(side, piece, 3).wait_recv()

        @pl.when(unit == 3)
        def _():
            def divide(item, inner):
                r = pl.multiple_of((side * PAIR * GROUP + item) * rows, rows)
                columns = pl.ds(pl.multiple_of(item * HEAD_SIZE, HEAD_SIZE), HEAD_SIZE)
                for who in range(2):
                    part = pl.ds(r + who * half, half)
                    result[who, side, :, columns] = (acc[part, :] / total[part, :]).astype(jnp.bfloat16)
                return inner

            lax.fori_loop(0, PAIR * GROUP, divide, 0)

        for of_side in range(2):

            @pl.when(number == 6 + of_side)
            def _(of_side=of_side):
                give_back(of_side).start()
                keep(of_side).start()

        return carry

    lax.fori_loop(0, 8, phase, 0)

    put_short.wait()
    for side in range(2):
        keep(side).wait()
        give_back(side).wait_recv()
        give_back(side).wait_send()
        mate_kv(side).wait_send()
        for which in range(4):
            near(side, which).wait_send()
            for piece in range(SIDE):
                far(side, piece, which).wait_send()
    mate_q().wait_send()


def on_device(long_query, long_kv, short_query, short_key_value, short_seg):
    half, tokens = long_query.shape[0], short_query.shape[0]
    rows = 2 * half
    state_rows = LOCAL_HEADS * GROUP * rows
    seg_row = jnp.broadcast_to(short_seg, (8, tokens))
    seg_col = jnp.broadcast_to(short_seg.reshape(tokens, 1), (tokens, HEAD_SIZE))
    anywhere = pl.BlockSpec(memory_space=pl.ANY)
    vmem = pl.BlockSpec(memory_space=pltpu.VMEM)
    return pl.pallas_call(
        kernel,
        out_shape=(
            jax.ShapeDtypeStruct(long_query.shape, long_query.dtype),
            jax.ShapeDtypeStruct(short_query.shape, short_query.dtype),
        ),
        in_specs=[anywhere] * 4 + [vmem] * 2,
        out_specs=(anywhere, anywhere),
        scratch_shapes=[
            pltpu.VMEM((2, half, LOCAL_HEADS * WIDE), jnp.bfloat16),
            pltpu.VMEM((2, 4, 2, SIDE, rows, PAIR_WIDTH), jnp.bfloat16),
            pltpu.VMEM((state_rows, HEAD_SIZE), jnp.float32),
            pltpu.VMEM((state_rows, HEAD_SIZE), jnp.float32),
            pltpu.VMEM((state_rows, HEAD_SIZE), jnp.float32),
            pltpu.VMEM((rows, SIDE * rows), jnp.float32),
            pltpu.VMEM((rows, SIDE * rows), jnp.float32),
            pltpu.VMEM((2, 2, half, PAIR * WIDE), jnp.bfloat16),
            pltpu.VMEM(short_query.shape, jnp.bfloat16),
            pltpu.VMEM(short_key_value.shape, jnp.bfloat16),
            pltpu.SemaphoreType.DMA((COPIES,)),
            pltpu.SemaphoreType.DMA((COPIES,)),
            pltpu.SemaphoreType.DMA((8,)),
        ],
        compiler_params=pltpu.CompilerParams(
            collective_id=0, has_side_effects=True, vmem_limit_bytes=63 << 20
        ),
        name="window_attention",
    )(long_query, long_kv, short_query, short_key_value, seg_row, seg_col)


def solution(mesh):
    return jax.shard_map(
        on_device,
        mesh=mesh,
        in_specs=(
            P(("dp", "ctx", "head"), None),
            P(None, ("dp", "ctx", "head"), None),
            P(("dp", "ctx", "head"), None),
            P(None, ("dp", "ctx", "head"), None),
            P(("dp", "ctx", "head"), None),
        ),
        out_specs=(P(("dp", "ctx", "head"), None), P(("dp", "ctx", "head"), None)),
        check_vma=False,
    )
```

time: 656 us -> 173 us (0.26)
  the two profiles are of different devices: /device:TPU:89 before, /device:TPU:17 now
where the time goes in v2:
time: 173 us; the launch traced here: 172 us
  Pallas kernels  163 us (94%)
  local copies, waits for them, and re-layouts  8.74 us (5%)
    pallas_call x1, Pallas kernels, on_device(): pl.pallas_call(kernel, out_shape=(jax.ShapeDtypeStruct(long_query.shape,...  163 us
    unnamed x4, local copies, waits for them, and re-layouts  6.02 us

profile of v2, /device:TPU:17, one launch (start us, length us, event | category | flops | bytes accessed | tf_op | source)
XLA Modules:
  0.0 172.4 jit_solution(12782525522559229269)
XLA Ops:
  0.6 1.3 broadcast_in_dim.13.seg_row
  1.9 1.4 broadcast_in_dim.14.seg_col
  3.3 163.1 %window_attention.1 = (bf16[192,8192]{1,0:T(8,128)(2,1)}, bf16[256,8192]{1,0:T(8,128)(2,1)}) custom-call(bf16[192,8192]{1,0:T(8,128)(2,1)} %q_hbm.1, bf16[2,192,1024]{2,1,0:T(8,128)(2,1)} %kv_hbm.1, bf16[256,8192]{1,0:T(8,128)(2,1)} %short_q_hbm.1, bf16[2,256,1024]{2,1,0:T(8,128)(2,1)} %short_kv_hbm.1, s32[8,256]{1,0:T(8,128)} %broadcast_in_dim.13.seg_row, ...), custom_call_target="tpu_custom_call" | custom-call | tf_op jit(solution)/shard_map/window_attention/pallas_call | solution.py:340
  166.4 0.0 copy-start
  166.4 4.0 %copy.9 = bf16[192,8192]{1,0:T(8,128)(2,1)} copy(bf16[192,8192]{1,0:T(8,128)(2,1)} %get-tuple-element.4) | data formatting | bytes 6291456
  170.4 0.0 copy-done
  170.4 2.0 %copy.10 = bf16[256,8192]{1,0:T(8,128)(2,1)} copy(bf16[256,8192]{1,0:T(8,128)(2,1)S(1)} %copy-done) | data formatting | bytes 8388608
Async XLA Ops:
  166.4 4.0 %copy-start = (bf16[256,8192]{1,0:T(8,128)(2,1)S(1)}, bf16[256,8192]{1,0:T(8,128)(2,1)}, u32[]{:S(2)}) copy-start(bf16[256,8192]{1,0:T(8,128)(2,1)} %get-tuple-element.5) | copy-start | bytes 12582916

commit v3 on v2

--- a/solution.py
+++ b/solution.py
@@ -39,8 +39,8 @@
 
 
 def kernel(
-    q_hbm, kv_hbm, short_q_hbm, short_kv_hbm, seg_row, seg_col, out_hbm, short_out_hbm,
-    q, kv, acc, high, total, score_0, score_1, result, short_q, short_kv, send, recv, local,
+    q_hbm, kv_hbm, short_q_hbm, short_kv_hbm, seg, out_hbm, short_out_hbm,
+    q, kv, acc, high, total, result, short_q, short_kv, send, recv, local,
 ):
     half = q_hbm.shape[0]
     rows = 2 * half
@@ -84,16 +84,27 @@
             return remote(kv.at[side, 0, 0, 1], kv.at[side, 0, 0, 3], index, ahead[side])
         return remote(kv.at[side, 0, 1, 2], kv.at[side, 0, 1, 3], index, behind[side])
 
+    def from_behind(side, piece, at_y):
+        both = jnp.logical_or(side == 1, at_y == SIDE - 1)
+        return jnp.where(both, 1 + piece // 2, 1), jnp.where(both, 2 * (piece % 2), piece)
+
+    def from_ahead(side, piece, at_y):
+        both = jnp.logical_or(side == 1, at_y == SIDE - 1)
+        return jnp.where(both, 1 + piece // 2, 2), jnp.where(both, 2 * (piece % 2) + 1, piece)
+
     def far(side, piece, which):
         index = FAR + 16 * side + 4 * piece + which
-        unit, slot = 1 + piece // 2, 2 * (piece % 2)
         if which == 0:
+            unit, slot = from_behind(side, piece, wrap(y + 1))
             return remote(kv.at[side, 0, :, piece], kv.at[side, unit, :, slot], index, ahead[1 - side])
         if which == 1:
-            return remote(kv.at[side, 0, :, piece], kv.at[side, unit, :, slot + 1], index, behind[1 - side])
+            unit, slot = from_ahead(side, piece, wrap(y - 1))
+            return remote(kv.at[side, 0, :, piece], kv.at[side, unit, :, slot], index, behind[1 - side])
         if which == 2:
+            unit, slot = from_behind(side, piece, y)
             return remote(kv.at[side, unit, 0, slot], kv.at[side, 3, 0, piece], index, ahead[1 - side])
-        return remote(kv.at[side, unit, 1, slot + 1], kv.at[side, 3, 1, piece], index, behind[1 - side])
+        unit, slot = from_ahead(side, piece, y)
+        return remote(kv.at[side, unit, 1, slot], kv.at[side, 3, 1, piece], index, behind[1 - side])
 
     def give_back(side):
         columns = heads_of(core, side * (PAIR * WIDE), PAIR * WIDE)
@@ -135,6 +146,8 @@
 
     tokens = short_q.shape[0]
     part_rows = tokens // 2
+    seg_row = seg[...].astype(jnp.float32)
+    seg_col = jnp.broadcast_to(seg_row, (HEAD_SIZE, tokens)).T
 
     def short_head(g, carry):
         key_columns = pl.ds(pl.multiple_of(g * HEAD_SIZE, HEAD_SIZE), HEAD_SIZE)
@@ -194,10 +207,12 @@
         unit, side = lax.div(number, 2), lax.rem(number, 2)
         owners = []
         for slot in range(SIDE):
-            beyond = lax.div(slot, 2) + 2 * (unit - 1)
+            both = jnp.logical_or(side == 1, y == SIDE - 1)
+            beyond = jnp.where(both, slot // 2 + 2 * (unit - 1), slot)
             ring = jnp.where(jnp.logical_or(unit == 0, unit == 3), slot, beyond)
+            next_to = jnp.where(both, 2 * (slot % 2) - 1, 2 * unit - 3)
             along = jnp.where(ring == 1, -1, jnp.where(ring == 2, 1, jnp.where(ring == 3, 2, 0)))
-            across = jnp.where(unit == 0, 0, jnp.where(unit == 3, 2, 2 * (slot % 2) - 1))
+            across = jnp.where(unit == 0, 0, jnp.where(unit == 3, 2, next_to))
             owner_y = wrap(y + jnp.where(side == 0, across, along))
             owner_z = wrap(z + jnp.where(side == 0, along, across))
             owners.append(owner_y * SIDE + owner_z)
@@ -208,15 +223,12 @@
             columns = pl.ds(pl.multiple_of(local_head * HEAD_SIZE, HEAD_SIZE), HEAD_SIZE)
             return kv[side, unit, plane, :, :, columns].reshape(SIDE * rows, HEAD_SIZE)
 
-        def scores(item):
+        def scores(item, k):
             columns = pl.ds(pl.multiple_of((side * PAIR * GROUP + item) * HEAD_SIZE, HEAD_SIZE), HEAD_SIZE)
             query = jnp.concatenate([q[0, :, columns], q[1, :, columns]], axis=0)
-            return dot_nt(query, block(lax.div(item, GROUP), 0))
-
-        def update(item, score, masked, first):
-            v = block(lax.div(item, GROUP), 1)
-            v_one = jnp.concatenate([v, jnp.ones_like(v)], axis=1)
-            s = score[...]
+            return dot_nt(query, k)
+
+        def update(item, s, v_one, masked, first):
             if masked:
                 k_pos = jnp.concatenate([owner * rows + key_index for owner in owners], axis=1)
                 s = jnp.where(k_pos <= q_pos, s, NEG_LARGE)
@@ -239,18 +251,18 @@
                 total[r, :] = total[r, :] * factor + mixed[:, HEAD_SIZE:]
 
         def run(masked, first):
-            items = PAIR * GROUP
-            score_0[...] = scores(0)
-
-            def two(couple, inner):
-                item = couple * 2
-                score_1[...] = scores(item + 1)
-                update(item, score_0, masked, first)
-                score_0[...] = scores(jnp.minimum(item + 2, items - 1))
-                update(item + 1, score_1, masked, first)
+            def one_head(local_head, inner):
+                k, v = block(local_head, 0), block(local_head, 1)
+                v_one = jnp.concatenate([v, jnp.ones_like(v)], axis=1)
+                start = local_head * GROUP
+                s = scores(start, k)
+                for h in range(GROUP):
+                    ahead_s = scores(start + h + 1, k) if h + 1 < GROUP else None
+                    update(start + h, s, v_one, masked, first)
+                    s = ahead_s
                 return inner
 
-            lax.fori_loop(0, items // 2, two, 0)
+            lax.fori_loop(0, PAIR, one_head, 0)
 
         @pl.when(unit == 0)
         def _():
@@ -282,7 +294,7 @@
         def _():
             pass_on((1,))
 
-        @pl.when(number == 3)
+        @pl.when(number == jnp.where(y == SIDE - 1, 3, 1))
         def _():
             pass_on((2, 3))
 
@@ -330,11 +342,9 @@
 
 
 def on_device(long_query, long_kv, short_query, short_key_value, short_seg):
-    half, tokens = long_query.shape[0], short_query.shape[0]
+    half = long_query.shape[0]
     rows = 2 * half
     state_rows = LOCAL_HEADS * GROUP * rows
-    seg_row = jnp.broadcast_to(short_seg, (8, tokens))
-    seg_col = jnp.broadcast_to(short_seg.reshape(tokens, 1), (tokens, HEAD_SIZE))
     anywhere = pl.BlockSpec(memory_space=pl.ANY)
     vmem = pl.BlockSpec(memory_space=pltpu.VMEM)
     return pl.pallas_call(
@@ -343,7 +353,7 @@
             jax.ShapeDtypeStruct(long_query.shape, long_query.dtype),
             jax.ShapeDtypeStruct(short_query.shape, short_query.dtype),
         ),
-        in_specs=[anywhere] * 4 + [vmem] * 2,
+        in_specs=[anywhere] * 4 + [vmem],
         out_specs=(anywhere, anywhere),
         scratch_shapes=[
             pltpu.VMEM((2, half, LOCAL_HEADS * WIDE), jnp.bfloat16),
@@ -351,8 +361,6 @@
             pltpu.VMEM((state_rows, HEAD_SIZE), jnp.float32),
             pltpu.VMEM((state_rows, HEAD_SIZE), jnp.float32),
             pltpu.VMEM((state_rows, HEAD_SIZE), jnp.float32),
-            pltpu.VMEM((rows, SIDE * rows), jnp.float32),
-            pltpu.VMEM((rows, SIDE * rows), jnp.float32),
             pltpu.VMEM((2, 2, half, PAIR * WIDE), jnp.bfloat16),
             pltpu.VMEM(short_query.shape, jnp.bfloat16),
             pltpu.VMEM(short_key_value.shape, jnp.bfloat16),
@@ -364,7 +372,7 @@
             collective_id=0, has_side_effects=True, vmem_limit_bytes=63 << 20
         ),
         name="window_attention",
-    )(long_query, long_kv, short_query, short_key_value, seg_row, seg_col)
+    )(long_query, long_kv, short_query, short_key_value, short_seg)
 
 
 def solution(mesh):

time: 173 us -> 142 us (0.82)
  the two profiles are of different devices: /device:TPU:17 before, /device:TPU:25 now
where the time goes in v3:
time: 142 us; the launch traced here: 141 us
  Pallas kernels  135 us (95%)
  local copies, waits for them, and re-layouts  6.02 us (4%)
    pallas_call x1, Pallas kernels, on_device(): pl.pallas_call(kernel, out_shape=(jax.ShapeDtypeStruct(long_query.shape,...  135 us
    unnamed x4, local copies, waits for them, and re-layouts  6.02 us

profile of v3, /device:TPU:25, one launch (start us, length us, event | category | flops | bytes accessed | tf_op | source)
XLA Modules:
  0.0 141.4 jit_solution(15726022665606357413)
XLA Ops:
  0.6 134.8 %window_attention.1 = (bf16[192,8192]{1,0:T(8,128)(2,1)}, bf16[256,8192]{1,0:T(8,128)(2,1)}) custom-call(bf16[192,8192]{1,0:T(8,128)(2,1)} %q_hbm.1, bf16[2,192,1024]{2,1,0:T(8,128)(2,1)} %kv_hbm.1, bf16[256,8192]{1,0:T(8,128)(2,1)} %short_q_hbm.1, bf16[2,256,1024]{2,1,0:T(8,128)(2,1)} %short_kv_hbm.1, s32[1,256]{1,0:T(1,128)} %seg.1), custom_call_target="tpu_custom_call" | custom-call | tf_op jit(solution)/shard_map/window_attention/pallas_call | solution.py:350
  135.4 0.0 copy-start
  135.4 4.0 %copy.9 = bf16[192,8192]{1,0:T(8,128)(2,1)} copy(bf16[192,8192]{1,0:T(8,128)(2,1)} %get-tuple-element.4) | data formatting | bytes 6291456
  139.4 0.0 copy-done
  139.4 2.0 %copy.10 = bf16[256,8192]{1,0:T(8,128)(2,1)} copy(bf16[256,8192]{1,0:T(8,128)(2,1)S(1)} %copy-done) | data formatting | bytes 8388608
Async XLA Ops:
  135.4 4.0 %copy-start = (bf16[256,8192]{1,0:T(8,128)(2,1)S(1)}, bf16[256,8192]{1,0:T(8,128)(2,1)}, u32[]{:S(2)}) copy-start(bf16[256,8192]{1,0:T(8,128)(2,1)} %get-tuple-element.5) | copy-start | bytes 12582916

commit v4 on v3

--- a/solution.py
+++ b/solution.py
@@ -125,6 +125,9 @@
 
     own_kv[0].start()
     own_kv[1].start()
+    get_short_kv.start()
+    get_short_q.start()
+    own_q.start()
     barrier = pltpu.get_barrier_semaphore()
     for target in (mate,) + ahead + behind:
         pl.semaphore_signal(barrier, inc=1, device_id=target, device_id_type=MESH)
@@ -132,18 +135,11 @@
     for side in range(2):
         mate_kv(side).start()
     mate_q().start()
-    get_short_kv.start()
-    get_short_q.start()
-    own_q.start()
     for side in range(2):
         own_kv[side].wait()
         mate_kv(side).wait_recv()
         near(side, 0).start()
         near(side, 1).start()
-    for side in range(2):
-        far(side, 0, 0).start()
-        far(side, 0, 1).start()
-
     tokens = short_q.shape[0]
     part_rows = tokens // 2
     seg_row = seg[...].astype(jnp.float32)
@@ -183,7 +179,7 @@
                 near(side, 2).start()
                 near(side, 1).wait_recv()
                 near(side, 3).start()
-            for piece in (1, 2):
+            for piece in (0, 1, 2):
                 for side in range(2):
                     far(side, piece, 0).start()
                     far(side, piece, 1).start()
@@ -251,18 +247,23 @@
                 total[r, :] = total[r, :] * factor + mixed[:, HEAD_SIZE:]
 
         def run(masked, first):
-            def one_head(local_head, inner):
-                k, v = block(local_head, 0), block(local_head, 1)
-                v_one = jnp.concatenate([v, jnp.ones_like(v)], axis=1)
-                start = local_head * GROUP
-                s = scores(start, k)
-                for h in range(GROUP):
-                    ahead_s = scores(start + h + 1, k) if h + 1 < GROUP else None
-                    update(start + h, s, v_one, masked, first)
+            def some_heads(turn, inner):
+                count = GROUP if masked else PAIR * GROUP
+                start = turn * GROUP
+                s = scores(start, block(turn, 0))
+                for h in range(count):
+                    local_head = turn + h // GROUP
+                    following = turn + (h + 1) // GROUP
+                    ahead_s = scores(start + h + 1, block(following, 0)) if h + 1 < count else None
+                    v = block(local_head, 1)
+                    update(start + h, s, jnp.concatenate([v, jnp.ones_like(v)], axis=1), masked, first)
                     s = ahead_s
                 return inner
 
-            lax.fori_loop(0, PAIR, one_head, 0)
+            if masked:
+                lax.fori_loop(0, PAIR, some_heads, 0)
+            else:
+                some_heads(0, 0)
 
         @pl.when(unit == 0)
         def _():

time: 142 us -> 136 us (0.958)
  Pallas kernels: 135 us -> 129 us
    pallas_call x1, Pallas kernels: 135 us -> 129 us  [on_device(): pl.pallas_call(kernel, out_shape=(jax.ShapeDtypeStruct(long_query.shape,...]
where the time goes in v4:
time: 136 us
  Pallas kernels  129 us (95%)
  local copies, waits for them, and re-layouts  6.02 us (4%)
    pallas_call x1, Pallas kernels, on_device(): pl.pallas_call(kernel, out_shape=(jax.ShapeDtypeStruct(long_query.shape,...  129 us
    unnamed x4, local copies, waits for them, and re-layouts  6.02 us

profile of v4, /device:TPU:25, one launch (start us, length us, event | category | flops | bytes accessed | tf_op | source)
XLA Modules:
  0.0 135.5 jit_solution(11490661645337895009)
XLA Ops:
  0.6 128.9 %window_attention.1 = (bf16[192,8192]{1,0:T(8,128)(2,1)}, bf16[256,8192]{1,0:T(8,128)(2,1)}) custom-call(bf16[192,8192]{1,0:T(8,128)(2,1)} %q_hbm.1, bf16[2,192,1024]{2,1,0:T(8,128)(2,1)} %kv_hbm.1, bf16[256,8192]{1,0:T(8,128)(2,1)} %short_q_hbm.1, bf16[2,256,1024]{2,1,0:T(8,128)(2,1)} %short_kv_hbm.1, s32[1,256]{1,0:T(1,128)} %seg.1), custom_call_target="tpu_custom_call" | custom-call | tf_op jit(solution)/shard_map/window_attention/pallas_call | solution.py:351
  129.5 0.0 copy-start
  129.5 4.0 %copy.9 = bf16[192,8192]{1,0:T(8,128)(2,1)} copy(bf16[192,8192]{1,0:T(8,128)(2,1)} %get-tuple-element.4) | data formatting | bytes 6291456
  133.5 0.0 copy-done
  133.5 2.0 %copy.10 = bf16[256,8192]{1,0:T(8,128)(2,1)} copy(bf16[256,8192]{1,0:T(8,128)(2,1)S(1)} %copy-done) | data formatting | bytes 8388608
Async XLA Ops:
  129.5 4.0 %copy-start = (bf16[256,8192]{1,0:T(8,128)(2,1)S(1)}, bf16[256,8192]{1,0:T(8,128)(2,1)}, u32[]{:S(2)}) copy-start(bf16[256,8192]{1,0:T(8,128)(2,1)} %get-tuple-element.5) | copy-start | bytes 12582916

commit v5 on v4

--- a/solution.py
+++ b/solution.py
@@ -23,7 +23,10 @@
 PAIR_WIDTH = PAIR * HEAD_SIZE
 MESH = pl.DeviceIdType.MESH
 
-NEAR, FAR, RESULT, COPIES = 3, 11, 43, 45
+NEAR, FAR, RESULT, SHARE, COPIES = 3, 11, 43, 45, 48
+
+SHARED = 4
+KEPT = PAIR * GROUP - SHARED
 
 
 def dot_nt(a, b):
@@ -40,7 +43,7 @@
 
 def kernel(
     q_hbm, kv_hbm, short_q_hbm, short_kv_hbm, seg, out_hbm, short_out_hbm,
-    q, kv, acc, high, total, result, short_q, short_kv, send, recv, local,
+    q, kv, acc, high, total, result, q_extra, result_extra, short_q, short_kv, send, recv, local,
 ):
     half = q_hbm.shape[0]
     rows = 2 * half
@@ -66,7 +69,7 @@
         return pl.ds(pl.multiple_of(start, PAIR_WIDTH), PAIR_WIDTH)
 
     def heads_of(of_core, start, size):
-        return pl.ds(pl.multiple_of(of_core * q_columns + start, size), size)
+        return pl.ds(pl.multiple_of(of_core * q_columns + start, SHARED * HEAD_SIZE), size)
 
     def mate_kv(side):
         return remote(kv_hbm.at[:, :, mine_columns(side, 1 - core)], kv.at[side, 0, :, 0, pl.ds(half, half)], 1 + side, mate)
@@ -106,13 +109,24 @@
         unit, slot = from_ahead(side, piece, y)
         return remote(kv.at[side, unit, 1, slot], kv.at[side, 3, 1, piece], index, behind[1 - side])
 
-    def give_back(side):
-        columns = heads_of(core, side * (PAIR * WIDE), PAIR * WIDE)
-        return remote(result.at[1, side], out_hbm.at[:, columns], RESULT + side, mate)
-
-    def keep(side):
-        columns = heads_of(core, side * (PAIR * WIDE), PAIR * WIDE)
-        return pltpu.make_async_copy(result.at[0, side], out_hbm.at[:, columns], local.at[5 + side])
+    def give_back(side, width):
+        columns = heads_of(core, side * (PAIR * WIDE), width)
+        return remote(result.at[1, side, :, pl.ds(0, width)], out_hbm.at[:, columns], RESULT + side, mate)
+
+    def keep(side, width):
+        columns = heads_of(core, side * (PAIR * WIDE), width)
+        return pltpu.make_async_copy(result.at[0, side, :, pl.ds(0, width)], out_hbm.at[:, columns], local.at[5 + side])
+
+    gives, takes = y == SIDE - 1, y == 0
+    whole, part_width = PAIR * WIDE, KEPT * HEAD_SIZE
+
+    def share_q():
+        return remote(q.at[:, :, pl.ds(part_width, SHARED * HEAD_SIZE)], q_extra, SHARE, ahead[1])
+
+    def share_result(who):
+        columns = heads_of(core, part_width, SHARED * HEAD_SIZE)
+        target = behind[1] if who == 0 else device(wrap(y - 1), z, 1 - core)
+        return remote(result_extra.at[who], out_hbm.at[:, columns], SHARE + 1 + who, target)
 
     own_q = pltpu.make_async_copy(q_hbm.at[:, heads_of(core, 0, q_columns)], q.at[0], local.at[0])
     own_kv = [
@@ -129,9 +143,10 @@
     get_short_q.start()
     own_q.start()
     barrier = pltpu.get_barrier_semaphore()
-    for target in (mate,) + ahead + behind:
+    crossed = (device(wrap(y + 1), z, 1 - core), device(wrap(y - 1), z, 1 - core))
+    for target in (mate,) + ahead + behind + crossed:
         pl.semaphore_signal(barrier, inc=1, device_id=target, device_id_type=MESH)
-    pl.semaphore_wait(barrier, 5)
+    pl.semaphore_wait(barrier, 7)
     for side in range(2):
         mate_kv(side).start()
     mate_q().start()
@@ -190,6 +205,11 @@
     put_short.start()
     own_q.wait()
     mate_q().wait_recv()
+
+    @pl.when(gives)
+    def _():
+        share_q().start()
+
     for side in range(2):
         near(side, 2).wait_recv()
         near(side, 3).wait_recv()
@@ -199,8 +219,7 @@
     q_pos = chip * rows + order_of(lax.broadcasted_iota(jnp.int32, (rows, 1), 0), half, core)
     key_index = order_of(lax.broadcasted_iota(jnp.int32, (1, rows), 1), half, core)
 
-    def phase(number, carry):
-        unit, side = lax.div(number, 2), lax.rem(number, 2)
+    def owners_of(unit, side):
         owners = []
         for slot in range(SIDE):
             both = jnp.logical_or(side == 1, y == SIDE - 1)
@@ -212,23 +231,30 @@
             owner_y = wrap(y + jnp.where(side == 0, across, along))
             owner_z = wrap(z + jnp.where(side == 0, along, across))
             owners.append(owner_y * SIDE + owner_z)
+        return owners
+
+    def phase(number, carry):
+        unit = lax.div(number, 2)
+        side = jnp.where(unit == 1, 1 - lax.rem(number, 2), lax.rem(number, 2))
+        owners = owners_of(unit, side)
         low = jnp.minimum(jnp.minimum(owners[0], owners[1]), jnp.minimum(owners[2], owners[3]))
         top = jnp.maximum(jnp.maximum(owners[0], owners[1]), jnp.maximum(owners[2], owners[3]))
 
-        def block(local_head, plane):
+        def block(local_head, plane, of_side=side, of_unit=unit):
             columns = pl.ds(pl.multiple_of(local_head * HEAD_SIZE, HEAD_SIZE), HEAD_SIZE)
-            return kv[side, unit, plane, :, :, columns].reshape(SIDE * rows, HEAD_SIZE)
+            return kv[of_side, of_unit, plane, :, :, columns].reshape(SIDE * rows, HEAD_SIZE)
 
         def scores(item, k):
             columns = pl.ds(pl.multiple_of((side * PAIR * GROUP + item) * HEAD_SIZE, HEAD_SIZE), HEAD_SIZE)
             query = jnp.concatenate([q[0, :, columns], q[1, :, columns]], axis=0)
             return dot_nt(query, k)
 
-        def update(item, s, v_one, masked, first):
-            if masked:
+        def update(place, s, v, owners, positions, first):
+            v_one = jnp.concatenate([v, jnp.ones_like(v)], axis=1)
+            if owners is not None:
                 k_pos = jnp.concatenate([owner * rows + key_index for owner in owners], axis=1)
-                s = jnp.where(k_pos <= q_pos, s, NEG_LARGE)
-            r = pl.ds(pl.multiple_of((side * PAIR * GROUP + item) * rows, rows), rows)
+                s = jnp.where(k_pos <= positions, s, NEG_LARGE)
+            r = pl.ds(pl.multiple_of(place * rows, rows), rows)
             best = jnp.max(s, axis=1, keepdims=True) * LOG2_SCALE
             if first:
                 new = jnp.broadcast_to(best, (rows, HEAD_SIZE))
@@ -246,17 +272,17 @@
                 acc[r, :] = acc[r, :] * factor + mixed[:, :HEAD_SIZE]
                 total[r, :] = total[r, :] * factor + mixed[:, HEAD_SIZE:]
 
-        def run(masked, first):
+        def run(masked, first, begin=0, straight=PAIR * GROUP):
             def some_heads(turn, inner):
-                count = GROUP if masked else PAIR * GROUP
-                start = turn * GROUP
-                s = scores(start, block(turn, 0))
+                count = GROUP if masked else straight
+                start = turn * GROUP + begin
+                s = scores(start, block(turn + begin // GROUP, 0))
                 for h in range(count):
-                    local_head = turn + h // GROUP
-                    following = turn + (h + 1) // GROUP
+                    local_head = turn + (begin + h) // GROUP
+                    following = turn + (begin + h + 1) // GROUP
                     ahead_s = scores(start + h + 1, block(following, 0)) if h + 1 < count else None
-                    v = block(local_head, 1)
-                    update(start + h, s, jnp.concatenate([v, jnp.ones_like(v)], axis=1), masked, first)
+                    place = side * PAIR * GROUP + start + h
+                    update(place, s, block(local_head, 1), owners if masked else None, q_pos, first)
                     s = ahead_s
                 return inner
 
@@ -271,9 +297,16 @@
 
         used = jnp.logical_and(unit > 0, low <= chip)
 
-        @pl.when(jnp.logical_and(used, top < chip))
-        def _():
-            run(False, False)
+        clear = jnp.logical_and(used, top < chip)
+        fewer = jnp.logical_and(gives, side == 0)
+
+        @pl.when(clear)
+        def _():
+            run(False, False, 0, KEPT)
+
+        @pl.when(jnp.logical_and(clear, jnp.logical_not(fewer)))
+        def _():
+            run(False, False, KEPT, SHARED)
 
         @pl.when(jnp.logical_and(used, top >= chip))
         def _():
@@ -295,7 +328,7 @@
         def _():
             pass_on((1,))
 
-        @pl.when(number == jnp.where(y == SIDE - 1, 3, 1))
+        @pl.when(number == jnp.where(y == SIDE - 1, 3, 2))
         def _():
             pass_on((2, 3))
 
@@ -305,6 +338,39 @@
                 for side in range(2):
                     far(side, piece, 2).wait_recv()
                     far(side, piece, 3).wait_recv()
+
+        extra = LOCAL_HEADS * GROUP
+
+        @pl.when(jnp.logical_and(takes, number == 3))
+        def _():
+            share_q().wait_recv()
+            area = pl.ds(extra * rows, SHARED * rows)
+            acc[area, :] = jnp.zeros((SHARED * rows, HEAD_SIZE), jnp.float32)
+            total[area, :] = jnp.zeros((SHARED * rows, HEAD_SIZE), jnp.float32)
+            high[area, :] = jnp.full((SHARED * rows, HEAD_SIZE), NEG_LARGE, jnp.float32)
+
+        @pl.when(jnp.logical_and(takes, jnp.logical_or(number == 3, number == 5)))
+        def _():
+            def shared_unit(of_unit, inner):
+                local_head = KEPT // GROUP
+                k, v = block(local_head, 0, 0, of_unit), block(local_head, 1, 0, of_unit)
+                positions = q_pos + (SIDE - 1) * SIDE * rows
+                for h in range(SHARED):
+                    columns = slice(h * HEAD_SIZE, (h + 1) * HEAD_SIZE)
+                    query = jnp.concatenate([q_extra[0, :, columns], q_extra[1, :, columns]], axis=0)
+                    update(extra + h, dot_nt(query, k), v, owners_of(of_unit, 0), positions, False)
+                return inner
+
+            lax.fori_loop(jnp.where(number == 3, 0, 3), jnp.where(number == 3, 3, 4), shared_unit, 0)
+
+        @pl.when(jnp.logical_and(takes, number == 5))
+        def _():
+            for h in range(SHARED):
+                for who in range(2):
+                    part = pl.ds((extra + h) * rows + who * half, half)
+                    result_extra[who, :, h * HEAD_SIZE : (h + 1) * HEAD_SIZE] = (acc[part, :] / total[part, :]).astype(jnp.bfloat16)
+            share_result(0).start()
+            share_result(1).start()
 
         @pl.when(unit == 3)
         def _():
@@ -318,22 +384,50 @@
 
             lax.fori_loop(0, PAIR * GROUP, divide, 0)
 
-        for of_side in range(2):
-
-            @pl.when(number == 6 + of_side)
-            def _(of_side=of_side):
-                give_back(of_side).start()
-                keep(of_side).start()
+        @pl.when(jnp.logical_and(number == 6, gives))
+        def _():
+            give_back(0, part_width).start()
+            keep(0, part_width).start()
+
+        @pl.when(jnp.logical_and(number == 6, jnp.logical_not(gives)))
+        def _():
+            give_back(0, whole).start()
+            keep(0, whole).start()
+
+        @pl.when(number == 7)
+        def _():
+            give_back(1, whole).start()
+            keep(1, whole).start()
 
         return carry
 
     lax.fori_loop(0, 8, phase, 0)
 
     put_short.wait()
+    def finish(side, width):
+        keep(side, width).wait()
+        give_back(side, width).wait_recv()
+        give_back(side, width).wait_send()
+
+    finish(1, whole)
+
+    @pl.when(gives)
+    def _():
+        finish(0, part_width)
+        share_q().wait_send()
+        share_result(0).wait_recv()
+        share_result(1).wait_recv()
+
+    @pl.when(jnp.logical_not(gives))
+    def _():
+        finish(0, whole)
+
+    @pl.when(takes)
+    def _():
+        share_result(0).wait_send()
+        share_result(1).wait_send()
+
     for side in range(2):
-        keep(side).wait()
-        give_back(side).wait_recv()
-        give_back(side).wait_send()
         mate_kv(side).wait_send()
         for which in range(4):
             near(side, which).wait_send()
@@ -345,7 +439,7 @@
 def on_device(long_query, long_kv, short_query, short_key_value, short_seg):
     half = long_query.shape[0]
     rows = 2 * half
-    state_rows = LOCAL_HEADS * GROUP * rows
+    state_rows = (LOCAL_HEADS * GROUP + SHARED) * rows
     anywhere = pl.BlockSpec(memory_space=pl.ANY)
     vmem = pl.BlockSpec(memory_space=pltpu.VMEM)
     return pl.pallas_call(
@@ -363,6 +457,8 @@
             pltpu.VMEM((state_rows, HEAD_SIZE), jnp.float32),
             pltpu.VMEM((state_rows, HEAD_SIZE), jnp.float32),
             pltpu.VMEM((2, 2, half, PAIR * WIDE), jnp.bfloat16),
+            pltpu.VMEM((2, half, SHARED * HEAD_SIZE), jnp.bfloat16),
+            pltpu.VMEM((2, half, SHARED * HEAD_SIZE), jnp.bfloat16),
             pltpu.VMEM(short_query.shape, jnp.bfloat16),
             pltpu.VMEM(short_key_value.shape, jnp.bfloat16),
             pltpu.SemaphoreType.DMA((COPIES,)),

time: 136 us -> 129 us (0.949)
  Pallas kernels: 129 us -> 122 us
    pallas_call x1, Pallas kernels: 129 us -> 122 us  [on_device(): pl.pallas_call(kernel, out_shape=(jax.ShapeDtypeStruct(long_query.shape,...]
where the time goes in v5:
time: 129 us; the launch traced here: 128 us
  Pallas kernels  122 us (95%)
  local copies, waits for them, and re-layouts  6.02 us (5%)
    pallas_call x1, Pallas kernels, on_device(): pl.pallas_call(kernel, out_shape=(jax.ShapeDtypeStruct(long_query.shape,...  122 us
    unnamed x4, local copies, waits for them, and re-layouts  6.02 us

profile of v5, /device:TPU:25, one launch (start us, length us, event | category | flops | bytes accessed | tf_op | source)
XLA Modules:
  0.0 128.4 jit_solution(9720809739733138963)
XLA Ops:
  0.6 121.7 %window_attention.1 = (bf16[192,8192]{1,0:T(8,128)(2,1)}, bf16[256,8192]{1,0:T(8,128)(2,1)}) custom-call(bf16[192,8192]{1,0:T(8,128)(2,1)} %q_hbm.1, bf16[2,192,1024]{2,1,0:T(8,128)(2,1)} %kv_hbm.1, bf16[256,8192]{1,0:T(8,128)(2,1)} %short_q_hbm.1, bf16[2,256,1024]{2,1,0:T(8,128)(2,1)} %short_kv_hbm.1, s32[1,256]{1,0:T(1,128)} %seg.1), custom_call_target="tpu_custom_call" | custom-call | tf_op jit(solution)/shard_map/window_attention/pallas_call | solution.py:445
  122.4 0.0 copy-start
  122.4 4.0 %copy.9 = bf16[192,8192]{1,0:T(8,128)(2,1)} copy(bf16[192,8192]{1,0:T(8,128)(2,1)} %get-tuple-element.4) | data formatting | bytes 6291456
  126.4 0.0 copy-done
  126.4 2.0 %copy.10 = bf16[256,8192]{1,0:T(8,128)(2,1)} copy(bf16[256,8192]{1,0:T(8,128)(2,1)S(1)} %copy-done) | data formatting | bytes 8388608
Async XLA Ops:
  122.4 4.0 %copy-start = (bf16[256,8192]{1,0:T(8,128)(2,1)S(1)}, bf16[256,8192]{1,0:T(8,128)(2,1)}, u32[]{:S(2)}) copy-start(bf16[256,8192]{1,0:T(8,128)(2,1)} %get-tuple-element.5) | copy-start | bytes 12582916

commit v6 on v5

--- a/solution.py
+++ b/solution.py
@@ -25,7 +25,7 @@
 
 NEAR, FAR, RESULT, SHARE, COPIES = 3, 11, 43, 45, 48
 
-SHARED = 4
+SHARED = 6
 KEPT = PAIR * GROUP - SHARED
 
 
@@ -69,7 +69,7 @@
         return pl.ds(pl.multiple_of(start, PAIR_WIDTH), PAIR_WIDTH)
 
     def heads_of(of_core, start, size):
-        return pl.ds(pl.multiple_of(of_core * q_columns + start, SHARED * HEAD_SIZE), size)
+        return pl.ds(pl.multiple_of(of_core * q_columns + start, 2 * HEAD_SIZE), size)
 
     def mate_kv(side):
         return remote(kv_hbm.at[:, :, mine_columns(side, 1 - core)], kv.at[side, 0, :, 0, pl.ds(half, half)], 1 + side, mate)
@@ -117,15 +117,16 @@
         columns = heads_of(core, side * (PAIR * WIDE), width)
         return pltpu.make_async_copy(result.at[0, side, :, pl.ds(0, width)], out_hbm.at[:, columns], local.at[5 + side])
 
-    gives, takes = y == SIDE - 1, y == 0
+    gives, takes = y >= SIDE // 2, y < SIDE // 2
+    partner, crossed = device(SIDE - 1 - y, z, core), device(SIDE - 1 - y, z, 1 - core)
     whole, part_width = PAIR * WIDE, KEPT * HEAD_SIZE
 
     def share_q():
-        return remote(q.at[:, :, pl.ds(part_width, SHARED * HEAD_SIZE)], q_extra, SHARE, ahead[1])
+        return remote(q.at[:, :, pl.ds(part_width, SHARED * HEAD_SIZE)], q_extra, SHARE, partner)
 
     def share_result(who):
         columns = heads_of(core, part_width, SHARED * HEAD_SIZE)
-        target = behind[1] if who == 0 else device(wrap(y - 1), z, 1 - core)
+        target = partner if who == 0 else crossed
         return remote(result_extra.at[who], out_hbm.at[:, columns], SHARE + 1 + who, target)
 
     own_q = pltpu.make_async_copy(q_hbm.at[:, heads_of(core, 0, q_columns)], q.at[0], local.at[0])
@@ -143,10 +144,9 @@
     get_short_q.start()
     own_q.start()
     barrier = pltpu.get_barrier_semaphore()
-    crossed = (device(wrap(y + 1), z, 1 - core), device(wrap(y - 1), z, 1 - core))
-    for target in (mate,) + ahead + behind + crossed:
+    for target in (mate, crossed) + ahead + behind:
         pl.semaphore_signal(barrier, inc=1, device_id=target, device_id_type=MESH)
-    pl.semaphore_wait(barrier, 7)
+    pl.semaphore_wait(barrier, 6)
     for side in range(2):
         mate_kv(side).start()
     mate_q().start()
@@ -206,15 +206,15 @@
     own_q.wait()
     mate_q().wait_recv()
 
-    @pl.when(gives)
-    def _():
-        share_q().start()
-
     for side in range(2):
         near(side, 2).wait_recv()
         near(side, 3).wait_recv()
         far(side, 3, 0).start()
         far(side, 3, 1).start()
+
+    @pl.when(gives)
+    def _():
+        share_q().start()
 
     q_pos = chip * rows + order_of(lax.broadcasted_iota(jnp.int32, (rows, 1), 0), half, core)
     key_index = order_of(lax.broadcasted_iota(jnp.int32, (1, rows), 1), half, core)
@@ -354,14 +354,21 @@
             def shared_unit(of_unit, inner):
                 local_head = KEPT // GROUP
                 k, v = block(local_head, 0, 0, of_unit), block(local_head, 1, 0, of_unit)
-                positions = q_pos + (SIDE - 1) * SIDE * rows
+                positions = q_pos + (SIDE - 1 - 2 * y) * SIDE * rows
+                of_row = owners_of(of_unit, 0)
+
+                def shared_scores(h):
+                    columns = slice(h * HEAD_SIZE, (h + 1) * HEAD_SIZE)
+                    return dot_nt(jnp.concatenate([q_extra[0, :, columns], q_extra[1, :, columns]], axis=0), k)
+
+                s = shared_scores(0)
                 for h in range(SHARED):
-                    columns = slice(h * HEAD_SIZE, (h + 1) * HEAD_SIZE)
-                    query = jnp.concatenate([q_extra[0, :, columns], q_extra[1, :, columns]], axis=0)
-                    update(extra + h, dot_nt(query, k), v, owners_of(of_unit, 0), positions, False)
+                    ahead_s = shared_scores(h + 1) if h + 1 < SHARED else None
+                    update(extra + h, s, v, of_row, positions, False)
+                    s = ahead_s
                 return inner
 
-            lax.fori_loop(jnp.where(number == 3, 0, 3), jnp.where(number == 3, 3, 4), shared_unit, 0)
+            lax.fori_loop(jnp.where(number == 3, 0, 3), jnp.where(number == 3, 3, jnp.where(y == 0, 4, 3)), shared_unit, 0)
 
         @pl.when(jnp.logical_and(takes, number == 5))
         def _():

time: 129 us -> 124 us (0.961)
  Pallas kernels: 122 us -> 118 us
    pallas_call x1, Pallas kernels: 122 us -> 118 us  [on_device(): pl.pallas_call(kernel, out_shape=(jax.ShapeDtypeStruct(long_query.shape,...]
where the time goes in v6:
time: 124 us
  Pallas kernels  118 us (95%)
  local copies, waits for them, and re-layouts  6.02 us (5%)
    pallas_call x1, Pallas kernels, on_device(): pl.pallas_call(kernel, out_shape=(jax.ShapeDtypeStruct(long_query.shape,...  118 us
    unnamed x4, local copies, waits for them, and re-layouts  6.02 us

profile of v6, /device:TPU:25, one launch (start us, length us, event | category | flops | bytes accessed | tf_op | source)
XLA Modules:
  0.0 124.2 jit_solution(16250637084535667244)
XLA Ops:
  0.6 117.5 %window_attention.1 = (bf16[192,8192]{1,0:T(8,128)(2,1)}, bf16[256,8192]{1,0:T(8,128)(2,1)}) custom-call(bf16[192,8192]{1,0:T(8,128)(2,1)} %q_hbm.1, bf16[2,192,1024]{2,1,0:T(8,128)(2,1)} %kv_hbm.1, bf16[256,8192]{1,0:T(8,128)(2,1)} %short_q_hbm.1, bf16[2,256,1024]{2,1,0:T(8,128)(2,1)} %short_kv_hbm.1, s32[1,256]{1,0:T(1,128)} %seg.1), custom_call_target="tpu_custom_call" | custom-call | tf_op jit(solution)/shard_map/window_attention/pallas_call | solution.py:452
  118.1 0.0 copy-start
  118.2 4.0 %copy.9 = bf16[192,8192]{1,0:T(8,128)(2,1)} copy(bf16[192,8192]{1,0:T(8,128)(2,1)} %get-tuple-element.4) | data formatting | bytes 6291456
  122.2 0.0 copy-done
  122.2 2.0 %copy.10 = bf16[256,8192]{1,0:T(8,128)(2,1)} copy(bf16[256,8192]{1,0:T(8,128)(2,1)S(1)} %copy-done) | data formatting | bytes 8388608
Async XLA Ops:
  118.1 4.0 %copy-start = (bf16[256,8192]{1,0:T(8,128)(2,1)S(1)}, bf16[256,8192]{1,0:T(8,128)(2,1)}, u32[]{:S(2)}) copy-start(bf16[256,8192]{1,0:T(8,128)(2,1)} %get-tuple-element.5) | copy-start | bytes 12582916

commit v7 on v6

--- a/solution.py
+++ b/solution.py
@@ -23,7 +23,7 @@
 PAIR_WIDTH = PAIR * HEAD_SIZE
 MESH = pl.DeviceIdType.MESH
 
-NEAR, FAR, RESULT, SHARE, COPIES = 3, 11, 43, 45, 48
+NEAR, FAR, RESULT, SHARE, SECOND, COPIES = 3, 11, 43, 45, 48, 52
 
 SHARED = 6
 KEPT = PAIR * GROUP - SHARED
@@ -77,12 +77,14 @@
     def mate_q():
         return remote(q_hbm.at[:, heads_of(1 - core, 0, q_columns)], q.at[1], 0, mate)
 
+    def first_hop(side, which, part):
+        index = NEAR + 4 * side + which if part == 0 else SECOND + 2 * side + which
+        tokens = pl.ds(part * half, half)
+        target = ahead[side] if which == 0 else behind[side]
+        return remote(kv.at[side, 0, :, 0, tokens], kv.at[side, 0, :, 1 + which, tokens], index, target)
+
     def near(side, which):
         index = NEAR + 4 * side + which
-        if which == 0:
-            return remote(kv.at[side, 0, :, 0], kv.at[side, 0, :, 1], index, ahead[side])
-        if which == 1:
-            return remote(kv.at[side, 0, :, 0], kv.at[side, 0, :, 2], index, behind[side])
         if which == 2:
             return remote(kv.at[side, 0, 0, 1], kv.at[side, 0, 0, 3], index, ahead[side])
         return remote(kv.at[side, 0, 1, 2], kv.at[side, 0, 1, 3], index, behind[side])
@@ -152,9 +154,12 @@
     mate_q().start()
     for side in range(2):
         own_kv[side].wait()
+        first_hop(side, 0, 0).start()
+        first_hop(side, 1, 0).start()
+    for side in range(2):
         mate_kv(side).wait_recv()
-        near(side, 0).start()
-        near(side, 1).start()
+        first_hop(side, 0, 1).start()
+        first_hop(side, 1, 1).start()
     tokens = short_q.shape[0]
     part_rows = tokens // 2
     seg_row = seg[...].astype(jnp.float32)
@@ -190,9 +195,11 @@
         @pl.when(g == 5)
         def _():
             for side in range(2):
-                near(side, 0).wait_recv()
+                first_hop(side, 0, 0).wait_recv()
+                first_hop(side, 0, 1).wait_recv()
                 near(side, 2).start()
-                near(side, 1).wait_recv()
+                first_hop(side, 1, 0).wait_recv()
+                first_hop(side, 1, 1).wait_recv()
                 near(side, 3).start()
             for piece in (0, 1, 2):
                 for side in range(2):
@@ -436,8 +443,11 @@
 
     for side in range(2):
         mate_kv(side).wait_send()
+        for which in range(2):
+            first_hop(side, which, 0).wait_send()
+            first_hop(side, which, 1).wait_send()
+            near(side, 2 + which).wait_send()
         for which in range(4):
-            near(side, which).wait_send()
             for piece in range(SIDE):
                 far(side, piece, which).wait_send()
     mate_q().wait_send()

time: 124 us -> 123 us (level)
  Pallas kernels: 118 us -> 116 us
    pallas_call x1, Pallas kernels: 118 us -> 116 us  [on_device(): pl.pallas_call(kernel, out_shape=(jax.ShapeDtypeStruct(long_query.shape,...]
where the time goes in v7:
time: 123 us
  Pallas kernels  116 us (94%)
  local copies, waits for them, and re-layouts  6.02 us (5%)
    pallas_call x1, Pallas kernels, on_device(): pl.pallas_call(kernel, out_shape=(jax.ShapeDtypeStruct(long_query.shape,...  116 us
    unnamed x4, local copies, waits for them, and re-layouts  6.02 us

profile of v7, /device:TPU:25, one launch (start us, length us, event | category | flops | bytes accessed | tf_op | source)
XLA Modules:
  0.0 122.7 jit_solution(12583216014247772970)
XLA Ops:
  0.6 116.1 %window_attention.1 = (bf16[192,8192]{1,0:T(8,128)(2,1)}, bf16[256,8192]{1,0:T(8,128)(2,1)}) custom-call(bf16[192,8192]{1,0:T(8,128)(2,1)} %q_hbm.1, bf16[2,192,1024]{2,1,0:T(8,128)(2,1)} %kv_hbm.1, bf16[256,8192]{1,0:T(8,128)(2,1)} %short_q_hbm.1, bf16[2,256,1024]{2,1,0:T(8,128)(2,1)} %short_kv_hbm.1, s32[1,256]{1,0:T(1,128)} %seg.1), custom_call_target="tpu_custom_call" | custom-call | tf_op jit(solution)/shard_map/window_attention/pallas_call | solution.py:462
  116.7 0.0 copy-start
  116.7 4.0 %copy.9 = bf16[192,8192]{1,0:T(8,128)(2,1)} copy(bf16[192,8192]{1,0:T(8,128)(2,1)} %get-tuple-element.4) | data formatting | bytes 6291456
  120.7 0.0 copy-done
  120.7 2.0 %copy.10 = bf16[256,8192]{1,0:T(8,128)(2,1)} copy(bf16[256,8192]{1,0:T(8,128)(2,1)S(1)} %copy-done) | data formatting | bytes 8388608
Async XLA Ops:
  116.7 4.0 %copy-start = (bf16[256,8192]{1,0:T(8,128)(2,1)S(1)}, bf16[256,8192]{1,0:T(8,128)(2,1)}, u32[]{:S(2)}) copy-start(bf16[256,8192]{1,0:T(8,128)(2,1)} %get-tuple-element.5) | copy-start | bytes 12582916
